TPU v7x, 32 devices: a whole 2x2x4 slice. The times are simulated.
32 devices in a mesh: front: 8 (over y, x, core), panel: 4 (over z).
Axes of the slice: x: 2, y: 2, z: 4, core: 2. Of those that a mesh axis runs over, the one named last changes fastest.
Arguments:
- elem_tiles: bfloat16 [8, 4, 56, 128, 128], P('front', 'panel'), may hold values from -6 to 6
- targets: int32 [8, 4, 56, 1], P('front', 'panel'), may hold values from 0 to 7; in each aligned block of 56 rows (0 to 55, 56 to 111, ..., all dimensions but the last counted through in order) at most 14 rows name the same one
- tile_places: int32 [8, 4, 56], P('front', 'panel'), may hold values from 0 to 63, as said below
- friction: float32 [8, 2048], P('front'), may hold values from 0.25 to 4
Outputs:
- parent_half: float32 [8, 1536, 768], P('front', 'panel')
Inputs may be any that keep to these rules, and one draw needn't show every extreme that they name: `targets`: in the 56 tiles of one device at most 14 have the same target, and some target has exactly 14. `tile_places`: A place j * 16 + c of a tile on panel index p has j < 4 and c <= j * 4 + p, so tiles lie on or below the diagonal.
All inputs are finite; a program needn't handle non-finite values.
Results may differ from a plain program's by a relative error of at most 0.0003.
Values may be sent and summed in bfloat16 or wider, within the bound.
A program may use at most 128 MiB of HBM per device.

v0:
```python
import jax
import jax.numpy as jnp
from jax import lax
from jax.sharding import PartitionSpec as P


def from_partner(value, axis, apart):
    return lax.ppermute(value, axis, [(i, i ^ 1 << apart) for i in range(lax.axis_size(axis))])


def per_device(elem_tiles, targets, tile_places, friction):
    groups = lax.axis_size("front")
    panels = lax.axis_size("panel")
    count = elem_tiles.shape[2]
    edge = elem_tiles.shape[3]
    width = friction.shape[1]
    local_tiles = width // (edge * panels)
    col_tiles = width // edge
    panel_cols = edge * panels
    slots = max(2, (2 * count + groups - 1) // groups)
    flat = elem_tiles.reshape(count, edge * edge)
    target = targets.reshape(count)
    place = tile_places.reshape(count)
    hits = (target[:, None] == jnp.arange(groups, dtype=jnp.int32)[None, :]).astype(jnp.int32)
    before = jnp.cumsum(hits, axis=0) - hits
    rank = jnp.sum(before * hits, axis=1)
    slot_id = target * slots + rank
    picker = (jnp.arange(groups * slots, dtype=jnp.int32)[:, None] == slot_id[None, :]).astype(
        jnp.int32
    )
    filled = jnp.sum(picker, axis=1) > 0
    source_row = jnp.sum(picker * jnp.arange(count, dtype=jnp.int32)[None, :], axis=1)
    outgoing = jnp.where(
        filled[:, None], jnp.take(flat, source_row, axis=0), jnp.zeros((), jnp.bfloat16)
    )
    out_place = jnp.sum(picker * (place + 1)[None, :], axis=1)
    arrived, arrived_place = (
        lax.all_to_all(
            outgoing.reshape(groups, slots * edge * edge),
            "front",
            split_axis=0,
            concat_axis=0,
            tiled=True,
        ),
        lax.all_to_all(
            out_place.reshape(groups, slots), "front", split_axis=0, concat_axis=0, tiled=True
        ),
    )
    positions = local_tiles * col_tiles
    chooser = (
        jnp.arange(1, positions + 1, dtype=jnp.int32)[:, None] == arrived_place.reshape(-1)[None, :]
    ).astype(jnp.bfloat16)
    blocks = jnp.dot(
        chooser, arrived.reshape(groups * slots, edge * edge), preferred_element_type=jnp.float32
    )
    rows_here = local_tiles * edge
    lower = (
        blocks.reshape(local_tiles, col_tiles, edge, edge)
        .transpose(0, 2, 1, 3)
        .reshape(rows_here, width)
    )
    me_panel = lax.axis_index("panel")
    local_row = jnp.arange(rows_here, dtype=jnp.int32)
    global_row = (local_row // edge * panels + me_panel) * edge + local_row % edge
    lower = jnp.where(jnp.arange(width, dtype=jnp.int32)[None, :] < global_row[:, None], lower, 0.0)
    lower_b = lower.astype(jnp.bfloat16)
    fric_row = friction[0]
    sch_rows = (local_tiles - 1) * edge
    below_mine = lower_b[edge:]
    head_rows = lax.all_gather(lower_b[:edge, :panel_cols], "panel", axis=0, tiled=True)
    head_gram = jnp.dot(head_rows, head_rows.T, preferred_element_type=jnp.float32) / width
    factor = jnp.linalg.cholesky(head_gram + jnp.diag(fric_row[:panel_cols]))

    def solve_rows(rows):
        coupling = (
            jnp.dot(rows[:, :panel_cols], head_rows.T, preferred_element_type=jnp.float32) / width
        )
        return jax.scipy.linalg.solve_triangular(factor, coupling.T, lower=True).T

    solved_mine = solve_rows(below_mine)
    piece = lax.all_gather(below_mine, "panel", axis=0, tiled=True)
    gram_part = jnp.dot(below_mine, piece.T, preferred_element_type=jnp.float32) / width
    schur_core = gram_part - jnp.dot(
        solved_mine, solve_rows(piece).T, precision=lax.Precision.HIGHEST
    )
    column_pos = jnp.arange(panels * sch_rows, dtype=jnp.int32)
    row_pos = jnp.arange(sch_rows, dtype=jnp.int32)
    on_diagonal = column_pos[None, :] == (me_panel * sch_rows + row_pos)[:, None]
    schur = schur_core + jnp.where(on_diagonal, fric_row[global_row[edge:]][:, None], 0.0)
    row_orig = global_row[edge:] - panel_cols
    col_owner = column_pos // sch_rows
    col_tile = column_pos // edge % (local_tiles - 1)
    col_orig = (col_tile * panels + col_owner) * edge + column_pos % edge
    schur = jnp.where(col_orig[None, :] <= row_orig[:, None], schur, 0.0)
    half_cols = schur.shape[1] // 2
    side = lax.axis_index("front") % 2
    keep = lax.dynamic_slice_in_dim(schur, side * half_cols, half_cols, 1)
    other = lax.dynamic_slice_in_dim(schur, (1 - side) * half_cols, half_cols, 1)
    partner = from_partner(other, "front", 0)
    return (keep + partner)[None]


def solution(mesh):
    return jax.shard_map(
        per_device,
        mesh=mesh,
        in_specs=(
            P("front", "panel", None, None, None),
            P("front", "panel", None, None),
            P("front", "panel", None),
            P("front", None),
        ),
        out_specs=P("front", "panel", None),
        check_vma=False,
    )
```

profile of v0, /device:TPU:11, one launch (start us, length us, event | category | flops | bytes accessed | tf_op | source)
XLA Modules:
  0.0 366.2 jit_solution(1726774166854168227)
XLA Ops:
  6.5 0.7 add_bitcast_fusion.1
  7.2 0.7 fusion.74
  8.0 0.8 select_reduce_fusion.6
  8.8 0.7 multiply_add_fusion
  9.6 0.7 all_to_all.10
  10.3 4.5 %all-to-all-start = ((s32[8,1,14]{2,1,0:T(1,128)}), s32[8,1,14]{2,1,0:T(1,128)S(1)}, u32[]{:S(2)}, u32[]{:S(2)}) async-start(s32[8,1,14]{2,1,0:T(1,128)} %bitcast.2), calls=%async_computation | async-start | bytes 8192 | tf_op jit(solution)/shard_map/all_to_all | solution.py:45
  15.2 2.7 copy.38
  17.9 4.7 %gather_fusion = bf16[112,16384]{1,0:T(8,128)(2,1)} fusion(bf16[56,16384]{1,0:T(8,128)(2,1)S(1)} %bitcast.102, s32[1024]{0:T(1024)S(1)} %pad_clamp_fusion.1), kind=kCustom, calls=%fused_computation | custom fusion | bytes 7340480 | tf_op jit(solution)/shard_map/jit(_take)/gather | solution.py:34
  22.6 9.3 %gather.16 = bf16[8,1,229376]{2,0,1:T(8,128)(2,1)} reshape(bf16[112,16384]{1,0:T(8,128)(2,1)} %gather_fusion) | data formatting | bytes 7340032 | tf_op jit(solution)/shard_map/jit(_take)/gather | solution.py:34
  33.0 0.9 copy-done.1
  34.0 2.2 select_select_fusion
  36.7 6.0 %reduce.29 = bf16[8,229376]{1,0:T(8,128)(2,1)} reduce(bf16[8,1,229376]{2,0,1:T(8,128)(2,1)} %select_select_fusion, bf16[]{:T(256)} %broadcast.517), dimensions={1}, to_apply=%copy.25.reduce_sub_computation | reduce | bytes 7340034 | tf_op jit(solution)/shard_map/jit(_where)/select_n | solution.py:33
  42.8 7.3 %reshape.291 = bf16[8,2,114688]{2,1,0:T(2,128)(2,1)} reshape(bf16[8,229376]{1,0:T(8,128)(2,1)} %reduce.29) | data formatting | bytes 7340032
  50.0 4.5 %all-to-all-start.1 = ((bf16[8,2,114688]{2,1,0:T(2,128)(2,1)}), bf16[8,2,114688]{2,1,0:T(2,128)(2,1)}, u32[]{:S(2)}, u32[]{:S(2)}) async-start(bf16[8,2,114688]{2,1,0:T(2,128)(2,1)} %reshape.291), calls=%async_computation.1 | async-start | bytes 7340032 | tf_op jit(solution)/shard_map/all_to_all | solution.py:38
  55.1 0.7 reduce.28
  55.9 40.6 %all-to-all-done.1 = bf16[8,2,114688]{2,1,0:T(2,128)(2,1)} async-done(((bf16[8,2,114688]{2,1,0:T(2,128)(2,1)}), bf16[8,2,114688]{2,1,0:T(2,128)(2,1)}, u32[]{:S(2)}, u32[]{:S(2)}) %all-to-all-start.1) | async-done | bytes 3670048 | tf_op jit(solution)/shard_map/all_to_all | solution.py:38
  96.5 8.3 %reshape.292 = bf16[8,1,229376]{2,1,0:T(2,128)(2,1)} reshape(bf16[8,2,114688]{2,1,0:T(2,128)(2,1)} %all-to-all-done.1) | data formatting | bytes 7340032
  104.7 23.4 %reduce.25 = bf16[8,229376]{1,0:T(8,128)(2,1)} reduce(bf16[8,1,229376]{2,1,0:T(2,128)(2,1)} %reshape.292, bf16[]{:T(256)} %constant.322), dimensions={1}, to_apply=%all_to_all.12.reduce_sub_computation | reduce | bytes 7340034 | tf_op jit(solution)/shard_map/all_to_all | solution.py:38
  128.1 9.3 %reshape.241 = bf16[112,16384]{1,0:T(8,128)(2,1)} reshape(bf16[8,229376]{1,0:T(8,128)(2,1)} %reduce.25) | data formatting | bytes 7340032 | tf_op jit(solution)/shard_map/reshape | solution.py:54
  137.4 2.8 fusion.1
  140.2 0.7 fusion
  141.0 1.5 slice.189
  142.6 2.5 gather_fusion.1
  145.2 31.5 %all_gather.7 = bf16[512,512]{1,0:T(8,128)(2,1)S(1)} all-gather(bf16[128,512]{1,0:T(8,128)(2,1)S(1)} %slice.190), channel_id=1, replica_groups=mesh['front'=8,'panel'=4] {'panel'}, dimensions={0}, use_global_device_ids=true | all-gather | bytes 655360 | tf_op jit(solution)/shard_map/all_gather | solution.py:70
  177.8 1.0 copy-done.4
  178.8 11.7 %cholesky.103 = f32[128,128]{1,0:T(8,128)S(1)} custom-call(f32[128,128]{1,0:T(8,128)S(1)} %cholesky.263), custom_call_target="Cholesky" | custom-call | tf_op jit(solution)/shard_map/jit(cholesky)/cholesky | solution.py:72
  190.5 1.1 cholesky.222
  191.6 9.8 %custom-call.34 = f32[1,128,128]{1,2,0:T(8,128)S(1)} custom-call(f32[1,128,128]{2,1,0:T(8,128)S(1)} %get-tuple-element.35), custom_call_target="InvertDiagBlocksLowerTriangular" | custom-call | tf_op jit(solution)/shard_map/jit(cholesky)/cholesky | solution.py:72
  201.5 1.9 constant_dynamic-update-slice_fusion.2
  203.4 1.3 convolution_subtract_fusion.6
  204.7 11.7 %cholesky.215 = f32[128,128]{1,0:T(8,128)S(1)} custom-call(f32[128,128]{1,0:T(8,128)S(1)} %cholesky.267), custom_call_target="Cholesky" | custom-call | tf_op jit(solution)/shard_map/jit(cholesky)/cholesky | solution.py:72
  217.0 10.2 %custom-call.35 = f32[1,128,128]{1,2,0:T(8,128)S(1)} custom-call(f32[1,128,128]{2,1,0:T(8,128)S(1)} %get-tuple-element.32), custom_call_target="InvertDiagBlocksLowerTriangular" | custom-call | tf_op jit(solution)/shard_map/jit(cholesky)/cholesky | solution.py:72
  227.2 0.9 convolution_dynamic-update-slice_fusion
  228.1 1.6 convolution_subtract_fusion.7
  229.7 11.7 %cholesky.236 = f32[128,128]{1,0:T(8,128)S(1)} custom-call(f32[128,128]{1,0:T(8,128)S(1)} %cholesky.272), custom_call_target="Cholesky" | custom-call | tf_op jit(solution)/shard_map/jit(cholesky)/cholesky | solution.py:72
  242.1 9.8 %custom-call.36 = f32[1,128,128]{1,2,0:T(8,128)S(1)} custom-call(f32[1,128,128]{2,1,0:T(8,128)S(1)} %get-tuple-element.29), custom_call_target="InvertDiagBlocksLowerTriangular" | custom-call | tf_op jit(solution)/shard_map/jit(cholesky)/cholesky | solution.py:72
  251.9 0.8 convolution_dynamic-update-slice_fusion.1
  252.7 1.4 convolution_subtract_fusion.8
  254.1 11.9 %cholesky.253 = f32[128,128]{1,0:T(8,128)S(1)} custom-call(f32[128,128]{1,0:T(8,128)S(1)} %convolution_subtract_fusion.8), custom_call_target="Cholesky" | custom-call | tf_op jit(solution)/shard_map/jit(cholesky)/cholesky | solution.py:72
  266.0 0.6 compare_reduce_fusion.2
  270.7 2.3 select_select_fusion.1
  273.1 13.3 %while.1 = (s32[]{:T(128)}, f32[512,512]{1,0:T(8,128)}, s32[4,2]{0,1:T(2,128)S(1)}, f32[4,128,128]{2,1,0:T(8,128)}, s32[]{:T(128)}) while((s32[]{:T(128)}, f32[512,512]{1,0:T(8,128)}, s32[4,2]{0,1:T(2,128)S(1)}, f32[4,128,128]{2,1,0:T(8,128)}, s32[]{:T(128)}) %tuple.31), condition=%wide.while_cond, body=%wide.while_body.sunk | while | flops 2 | bytes 132205 | solution.py:78
  273.7 2.7 bitcast_dynamic-update-slice_fusion.2
  277.0 2.8 bitcast_dynamic-update-slice_fusion.2
  280.3 2.7 bitcast_dynamic-update-slice_fusion.2
  283.7 2.7 bitcast_dynamic-update-slice_fusion.2
  286.3 40.1 %custom-call.37 = f32[4,128,128]{1,2,0:T(8,128)S(1)} custom-call(f32[4,128,128]{2,1,0:T(8,128)} %get-tuple-element.12), custom_call_target="InvertDiagBlocksLowerTriangular" | custom-call | tf_op jit(solution)/shard_map/jit(_solve_triangular)/triangular_solve | solution.py:78
  327.3 1.2 convolution_subtract_fusion.5
  328.9 1.3 convolution_subtract_fusion.4
  330.5 1.5 convolution_subtract_fusion.3
  332.0 1.0 fusion.69
  333.1 2.4 convolution_multiply_fusion
  335.5 0.8 fusion.29
  336.4 2.0 convolution_subtract_fusion.2
  338.4 0.8 fusion.64
  339.3 2.0 convolution_subtract_fusion
  341.4 0.8 fusion.66
  342.2 2.5 convolution_subtract_fusion.1
  344.7 0.8 fusion.68
  345.6 2.9 convolution_multiply_fusion.1
  348.5 4.5 %fusion.17 = f32[384,1536]{1,0:T(8,128)S(1)} fusion(f32[384,1536]{1,0:T(8,128)S(1)} %convolution_multiply_fusion.1, f32[128,1536]{1,0:T(8,128)S(1)} %fusion.68, f32[128,1536]{1,0:T(8,128)S(1)} %fusion.66, f32[128,1536]{1,0:T(8,128)S(1)} %fusion.64, f32[128,1536]{1,0:T(8,128)S(1)} %fusion.29, f32[384]{0:T(512)S(1)} %gather_fusion.1, ...), kind=kOutput, calls=%fused_computation.23 | convolution fusion | flops 3630366720 | bytes 8661504 | tf_op jit(solution)/shard_map/dot_general | solution.py:83
  353.1 1.0 collective-permute-start
  354.0 2.6 collective-permute-done
  356.6 2.5 add_bitcast_fusion
  (69 shorter events, 11.2 us)
Async XLA Ops:
  10.3 39.8 %all-to-all-start = ((s32[8,1,14]{2,1,0:T(1,128)}), s32[8,1,14]{2,1,0:T(1,128)S(1)}, u32[]{:S(2)}, u32[]{:S(2)}) async-start(s32[8,1,14]{2,1,0:T(1,128)} %bitcast.2), calls=%async_computation | async-start | bytes 8192 | tf_op jit(solution)/shard_map/all_to_all | solution.py:45
  31.9 2.0 copy-start.1
  50.0 46.4 %all-to-all-start.1 = ((bf16[8,2,114688]{2,1,0:T(2,128)(2,1)}), bf16[8,2,114688]{2,1,0:T(2,128)(2,1)}, u32[]{:S(2)}, u32[]{:S(2)}) async-start(bf16[8,2,114688]{2,1,0:T(2,128)(2,1)} %reshape.291), calls=%async_computation.1 | async-start | bytes 7340032 | tf_op jit(solution)/shard_map/all_to_all | solution.py:38
  54.5 278.5 %all-gather.2.cloned.1.call-start = ((), (), s32[]{:S(2)}) async-start(), calls=%async_computation.2 | async-start | bytes 7864320 | tf_op jit(solution)/shard_map/all_gather | solution.py:81
  141.0 4.2 %copy-start.2 = (bf16[512,2048]{1,0:T(8,128)(2,1)}, bf16[512,2048]{1,0:T(8,128)(2,1)S(1)}, u32[]{:S(2)}) copy-start(bf16[512,2048]{1,0:T(8,128)(2,1)S(1)} %fusion) | copy-start | bytes 6291460
  141.0 1.5 copy-start
  177.8 1.0 copy-start.4
  228.1 98.4 %copy-start.3 = (bf16[512,2048]{1,0:T(8,128)(2,1)S(1)}, bf16[512,2048]{1,0:T(8,128)(2,1)}, u32[]{:S(2)}) copy-start(bf16[512,2048]{1,0:T(8,128)(2,1)} %copy-done.2) | copy-start | bytes 6291460
  335.5 10.0 %slice-start = ((s8[6291456]{0:T(1024)(128)(4,1)}), s8[4194304]{0:T(1024)(128)(4,1)S(1)}, s32[]{:S(2)}) async-start(s8[6291456]{0:T(1024)(128)(4,1)} %bitcast.108), calls=%async_computation.3 | async-start | bytes 8388608
  339.3 6.3 %slice-start.1 = ((s8[6291456]{0:T(1024)(128)(4,1)}), s8[2097152]{0:T(1024)(128)(4,1)S(1)}, s32[]{:S(2)}) async-start(s8[6291456]{0:T(1024)(128)(4,1)} %bitcast.108), calls=%async_computation.4 | async-start | bytes 4194304
  345.6 2.9 copy-start.5
  353.1 3.6 collective-permute-start
Sparse Core Ops, SparseCore 0:
  142.6 120.8 all-gather.1
where the time goes:
time: 373 us; the launch traced here: 366 us
  other arithmetic  162 us (43%)
  local copies, waits for them, and re-layouts  65.6 us (18%)
  waiting for transfers between devices  43.2 us (12%)
  matrix products  37.5 us (10%)
  blocking collectives  31.5 us (8%)
  between operations  16.4 us (4%)
  starting transfers between devices  10 us (3%)
    another operation x14, other arithmetic, per_device(): factor = jnp.linalg.cholesky(head_gram + jnp.diag(fric_row[:panel_cols]))  80.6 us
    another operation x3, other arithmetic, solve_rows(): return jax.scipy.linalg.solve_triangular(factor, coupling.T, lower=True).T  42.5 us
    all_to_all x1, waiting for transfers between devices, per_device(): lax.all_to_all(outgoing.reshape(groups, slots * edge * edge), 'front', sp...  40.6 us
    all_gather x1, blocking collectives, per_device(): lax.all_gather(lower_b[:edge, :panel_cols], 'panel', axis=0, tiled=True)  31.5 us
    all_to_all x1, other arithmetic, per_device(): lax.all_to_all(outgoing.reshape(groups, slots * edge * edge), 'front', sp...  23.4 us
    unnamed x19, local copies, waits for them, and re-layouts  20.2 us
    another operation x14, matrix products, solve_rows(): return jax.scipy.linalg.solve_triangular(factor, coupling.T, lower=True).T  16.1 us
    gather x2, local copies, waits for them, and re-layouts, per_device(): jnp.take(flat, source_row, axis=0)  14 us
  transfers between devices with their start and end apart: 4, of which 2 were waited for; matrix products, arithmetic and copies ran while one was open for 52% of the time, Pallas kernels for 0%

commit v1 on v0

v1 whole, which is shorter than its diff:
```python
import functools

import jax
import jax.numpy as jnp
from jax import lax
from jax.experimental import pallas as pl
from jax.experimental.pallas import tpu as pltpu
from jax.sharding import PartitionSpec as P

F32 = jnp.float32
BF16 = jnp.bfloat16
HEADER = 16
NN = (((1,), (0,)), ((), ()))
NT = (((1,), (1,)), ((), ()))
VMEM = pl.BlockSpec(memory_space=pltpu.VMEM)
SMEM = pl.BlockSpec(memory_space=pltpu.SMEM)


def split(x):
    hi = x.astype(BF16)
    return hi, (x - hi.astype(F32)).astype(BF16)


def dot(a, b, dims):
    return lax.dot_general(a, b, dims, preferred_element_type=F32)


def dot3(a, b, dims):
    ah, al = split(a)
    bh, bl = split(b)
    return dot(ah, bh, dims) + (dot(ah, bl, dims) + dot(al, bh, dims))


def pack_kernel(slots, target_ref, place_ref, tiles_ref, out_ref, count_ref, header_ref):
    tiles, edge = tiles_ref.shape[0], tiles_ref.shape[1]
    groups = out_ref.shape[0]
    header_ref[...] = jnp.zeros_like(header_ref)

    def clear(g, carry):
        count_ref[g] = 0
        return carry

    lax.fori_loop(0, groups, clear, 0)
    lane = lax.broadcasted_iota(jnp.int32, (1, edge), 1)

    def one(i, carry):
        t = target_ref[i]
        r = count_ref[t]
        count_ref[t] = r + 1
        out_ref[t, pl.ds(pl.multiple_of(r * edge, edge), edge), :] = tiles_ref[i]
        mark = (place_ref[i] + 1).astype(F32)
        header_ref[t] = jnp.where(lane == r, mark, header_ref[t])
        return carry

    lax.fori_loop(0, tiles, one, 0)

    def finish(g, carry):
        out_ref[g, pl.ds(slots * edge, HEADER), :] = jnp.broadcast_to(
            header_ref[g], (HEADER, edge)
        ).astype(BF16)
        return carry

    lax.fori_loop(0, groups, finish, 0)


def assemble_kernel(slots, panels, local_tiles, col_tiles, ids_ref, place_ref, arrived_ref, head_ref, below_ref, acc_ref):
    groups = arrived_ref.shape[0]
    edge = arrived_ref.shape[2]
    me = ids_ref[0]

    def clear(i, carry):
        acc_ref[i] = jnp.zeros((edge, edge), F32)
        return carry

    lax.fori_loop(0, local_tiles * col_tiles, clear, 0)

    def one_group(g, carry):
        def one(s, carry):
            place = place_ref[g, s]

            @pl.when(place > 0)
            def _():
                tile = arrived_ref[g, pl.ds(pl.multiple_of(s * edge, edge), edge), :]
                acc_ref[place - 1] += tile.astype(F32)

            return carry

        return lax.fori_loop(0, slots, one, carry)

    lax.fori_loop(0, groups, one_group, 0)
    row = lax.broadcasted_iota(jnp.int32, (edge, edge), 0)
    col = lax.broadcasted_iota(jnp.int32, (edge, edge), 1)
    start = 0
    for j in range(local_tiles):
        for c in range((j + 1) * panels):
            tile = acc_ref[j * col_tiles + c]
            if c >= j * panels:
                tile = jnp.where(c * edge + col < (j * panels + me) * edge + row, tile, 0.0)
            tile = tile.astype(BF16)
            if j == 0:
                head_ref[:, c * edge : (c + 1) * edge] = tile
            else:
                below_ref[:, start + c * edge : start + (c + 1) * edge] = tile
        if j > 0:
            start += (j + 1) * panels * edge


def invert_unit(block):
    edge = block.shape[0]
    count = edge // 8
    sub = lax.broadcasted_iota(jnp.int32, (8, edge), 0)
    lane = lax.broadcasted_iota(jnp.int32, (8, edge), 1)
    a = [block[8 * g : 8 * g + 8] for g in range(count)]
    e = [jnp.where(lane == sub + 8 * g, 1.0, 0.0).astype(F32) for g in range(count)]
    inv = [None] * count
    for k in range(edge):
        g, s = divmod(k, 8)
        a_row = a[g][s : s + 1]
        e_row = e[g][s : s + 1]
        pivot = jnp.broadcast_to(a_row[:, k : k + 1], (8, edge))
        flip = 1.0 / pivot
        inv[g] = flip if s == 0 else jnp.where(sub >= s, flip, inv[g])
        qa = jnp.broadcast_to(a_row, (8, edge)) * flip
        qe = jnp.broadcast_to(e_row, (8, edge)) * flip
        for i in range(g, count):
            if i == g and s == 7:
                continue
            column = jnp.broadcast_to(a[i][:, k : k + 1], (8, edge))
            if i == g:
                column = jnp.where(sub > s, column, 0.0)
            a[i] = a[i] - column * qa
            e[i] = e[i] - column * qe
    return jnp.concatenate(e, axis=0), jnp.concatenate(inv, axis=0)


def factor_kernel(width, head_ref, fric_ref, below_ref, high_ref, low_ref, a_ref, e_ref, d_ref):
    edge = below_ref.shape[0]
    order = head_ref.shape[0]
    blocks = order // edge
    head = head_ref[...]
    gram = dot(head, head, NT) * (1.0 / width)
    row = lax.broadcasted_iota(jnp.int32, (order, order), 0)
    col = lax.broadcasted_iota(jnp.int32, (order, order), 1)
    eye = row == col
    a_ref[...] = gram + jnp.where(eye, fric_ref[...], 0.0)
    e_ref[...] = jnp.where(eye, 1.0, 0.0).astype(F32)
    below_rows = lax.broadcasted_iota(jnp.int32, (order, 1), 0)

    def stage(b, carry):
        here = pl.ds(pl.multiple_of(b * edge, edge), edge)
        unit, flip = invert_unit(a_ref[here, here])
        up = dot3(unit, a_ref[here, :], NN)
        ue = dot3(unit, e_ref[here, :], NN)
        left = dot3(a_ref[:, here], unit, NT)
        left = jnp.where(below_rows >= (b + 1) * edge, left, 0.0)
        scale = jnp.concatenate([flip] * blocks, axis=1)
        e_ref[here, :] = ue
        d_ref[here, :] = scale
        a_ref[...] -= dot3(left, up * scale, NN)
        e_ref[...] -= dot3(left, ue * scale, NN)
        return carry

    lax.fori_loop(0, blocks, stage, 0)
    eh, el = split(e_ref[...])
    guess = dot(eh, head, NN) + dot(el, head, NN)
    gh, gl = split(guess)
    dh, dl = split(guess * (d_ref[...] * (1.0 / width)))
    start = 0
    for j in range(high_ref.shape[0] // edge):
        mine = below_ref[:, start : start + order]
        start += (j + 2) * order
        vh, vl = split(dot(mine, gh, NT) + dot(mine, gl, NT))
        done = mine.astype(F32) - (dot(vh, dh, NN) + (dot(vh, dl, NN) + dot(vl, dh, NN)))
        th, tl = split(done)
        high_ref[j * edge : (j + 1) * edge, :] = th
        low_ref[j * edge : (j + 1) * edge, :] = tl


def schur_kernel(width, panels, flip_side, ids_ref, high_ref, low_ref, below_ref, fric_ref, all_ref, out_ref):
    edge = below_ref.shape[0]
    order = high_ref.shape[1]
    rows = high_ref.shape[0] // edge
    half = panels // 2
    me = ids_ref[0]
    side = ids_ref[1]
    part = 1 - side if flip_side else side
    picked = pl.ds(pl.multiple_of(part * half * edge, edge), half * edge)
    starts = [0]
    for j in range(rows):
        starts.append(starts[-1] + (j + 2) * order)
    row = lax.broadcasted_iota(jnp.int32, (edge, edge), 0)
    col = lax.broadcasted_iota(jnp.int32, (edge, edge), 1)
    for jc in range(rows):
        first = starts[jc]
        last = first + (jc + 2) * order
        span = (jc + 1) * order
        theirs = all_ref[picked, first : first + order]
        rest = all_ref[picked, first + order : last]
        mine = jnp.concatenate(
            [below_ref[:, starts[j] + order : starts[j] + order + span] for j in range(jc, rows)], axis=0
        )
        total = dot(mine, rest, NT)
        total += dot(high_ref[jc * edge :, :], theirs, NT)
        total += dot(low_ref[jc * edge :, :], theirs, NT)
        total = total * (1.0 / width)
        for q in range(half):
            owner = part * half + q
            cols = slice(q * rows * edge + jc * edge, q * rows * edge + (jc + 1) * edge)
            for j in range(rows):
                if j < jc:
                    out_ref[j * edge : (j + 1) * edge, cols] = jnp.zeros((edge, edge), F32)
                    continue
                tile = total[(j - jc) * edge : (j - jc + 1) * edge, q * edge : (q + 1) * edge]
                if j == jc:
                    fric = fric_ref[(j + 1) * panels + me]
                    tile += jnp.where((row == col) & (owner == me), fric, 0.0)
                    tile = jnp.where(owner * edge + col <= me * edge + row, tile, 0.0)
                out_ref[j * edge : (j + 1) * edge, cols] = tile


def per_device(elem_tiles, targets, tile_places, friction):
    groups = lax.axis_size("front")
    panels = lax.axis_size("panel")
    count = elem_tiles.shape[2]
    edge = elem_tiles.shape[3]
    width = friction.shape[1]
    col_tiles = width // edge
    local_tiles = col_tiles // panels
    order = edge * panels
    slots = max(2, (2 * count + groups - 1) // groups)
    ids = jnp.stack([lax.axis_index("panel"), lax.axis_index("front") % 2]).astype(jnp.int32)

    packed = pl.pallas_call(
        functools.partial(pack_kernel, slots),
        out_shape=jax.ShapeDtypeStruct((groups, slots * edge + HEADER, edge), BF16),
        in_specs=[SMEM, SMEM, VMEM],
        out_specs=VMEM,
        scratch_shapes=[pltpu.SMEM((groups,), jnp.int32), pltpu.VMEM((groups, 1, edge), F32)],
        name="pack",
    )(targets.reshape(count), tile_places.reshape(count), elem_tiles.reshape(count, edge, edge))
    arrived = lax.all_to_all(packed, "front", split_axis=0, concat_axis=0, tiled=True)
    places = arrived[:, slots * edge, :slots].astype(jnp.int32)
    spread = sum((j + 1) * order for j in range(1, local_tiles))
    head, below = pl.pallas_call(
        functools.partial(assemble_kernel, slots, panels, local_tiles, col_tiles),
        out_shape=(
            jax.ShapeDtypeStruct((edge, order), BF16),
            jax.ShapeDtypeStruct((edge, spread), BF16),
        ),
        in_specs=[SMEM, SMEM, VMEM],
        out_specs=(VMEM, VMEM),
        scratch_shapes=[pltpu.VMEM((local_tiles * col_tiles, edge, edge), F32)],
        name="assemble",
    )(ids, places, arrived)
    head_rows = lax.all_gather(head, "panel", axis=0, tiled=True)
    all_rows = lax.all_gather(below, "panel", axis=0, tiled=True)
    rows = (local_tiles - 1) * edge
    high, low = pl.pallas_call(
        functools.partial(factor_kernel, width),
        out_shape=(
            jax.ShapeDtypeStruct((rows, order), BF16),
            jax.ShapeDtypeStruct((rows, order), BF16),
        ),
        in_specs=[VMEM, VMEM, VMEM],
        out_specs=(VMEM, VMEM),
        scratch_shapes=[pltpu.VMEM((order, order), F32)] * 3,
        cost_estimate=pl.CostEstimate(flops=30_000_000_000, bytes_accessed=4_000_000, transcendentals=0),
        name="factor",
    )(head_rows, friction[:, :order], below)

    def schur_half(flip_side):
        return pl.pallas_call(
            functools.partial(schur_kernel, width, panels, flip_side),
            out_shape=jax.ShapeDtypeStruct((rows, rows * panels // 2), F32),
            in_specs=[SMEM, VMEM, VMEM, VMEM, VMEM, VMEM],
            out_specs=VMEM,
            cost_estimate=pl.CostEstimate(flops=1_000_000_000, bytes_accessed=4_000_000, transcendentals=0),
            name="schur_other" if flip_side else "schur_keep",
        )(ids, high, low, below, friction.reshape(col_tiles, 1, edge), all_rows)

    other = schur_half(True)
    partner = lax.ppermute(other, "front", [(i, i ^ 1) for i in range(groups)])
    keep = schur_half(False)
    return (keep + partner)[None]


def solution(mesh):
    return jax.shard_map(
        per_device,
        mesh=mesh,
        in_specs=(
            P("front", "panel", None, None, None),
            P("front", "panel", None, None),
            P("front", "panel", None),
            P("front", None),
        ),
        out_specs=P("front", "panel", None),
        check_vma=False,
    )
```

time: 373 us -> 189 us (0.51); the launches traced: 366 us -> 187 us
  other arithmetic: 162 us -> 4.4 us
  Pallas kernels: 0 us -> 100 us
  local copies, waits for them, and re-layouts: 65.6 us -> 1.31 us
  matrix products: 37.5 us -> 0 us
  blocking collectives: 31.5 us -> 17.8 us
    another operation x18 -> x1, other arithmetic: 123 us -> 0.66 us  [per_device(): jnp.stack([lax.axis_index('panel'), lax.axis_index('front') % 2])]
    pallas_call x0 -> x5, Pallas kernels: none -> 100 us  [the longest x1 79.8 us: per_device(): pl.pallas_call(functools.partial(factor_kernel, width), out_shape=(jax.Sh...]
    all_to_all x2 -> x0, other arithmetic: 24.1 us -> none  [the longest x1 23.4 us: per_device(): lax.all_to_all(outgoing.reshape(groups, slots * edge * edge), 'front', sp...]
    another operation x20 -> x0, matrix products: 24 us -> none  [the longest x14 16.1 us: solve_rows(): return jax.scipy.linalg.solve_triangular(factor, coupling.T, lower=True).T]
    unnamed x19 -> x2, local copies, waits for them, and re-layouts: 20.2 us -> 0.01 us
    gather x3 -> x0, local copies, waits for them, and re-layouts: 16.5 us -> none  [the longest x2 14 us: per_device(): jnp.take(flat, source_row, axis=0)]
    another operation x17 -> x0, local copies, waits for them, and re-layouts: 14.4 us -> none
    all_gather x1, blocking collectives: 31.5 us -> 17.8 us  [per_device(): head_rows = lax.all_gather(head, 'panel', axis=0, tiled=True)]
  transfers between devices with their start and end apart: 4 -> 3, of which waited for: 2 -> 1; matrix products, arithmetic and copies ran while one was open for 52% -> 1% of each run, Pallas kernels for 0% -> 45%
where the time goes in v1:
time: 189 us; the launch traced here: 187 us
  Pallas kernels  100 us (53%)
  waiting for transfers between devices  41.7 us (22%)
  blocking collectives  17.8 us (9%)
  between operations  13.4 us (7%)
  starting transfers between devices  8.36 us (4%)
  other arithmetic  4.4 us (2%)
    pallas_call x1, Pallas kernels, per_device(): pl.pallas_call(functools.partial(factor_kernel, width), out_shape=(jax.Sh...  79.8 us
    all_to_all x1, waiting for transfers between devices, per_device(): lax.all_to_all(packed, 'front', split_axis=0, concat_axis=0, tiled=True)  41.7 us
    all_gather x1, blocking collectives, per_device(): head_rows = lax.all_gather(head, 'panel', axis=0, tiled=True)  17.8 us
    pallas_call x2, Pallas kernels, schur_half(): pl.pallas_call(functools.partial(schur_kernel, width, panels, flip_side),...  10.3 us
    pallas_call x1, Pallas kernels, per_device(): pl.pallas_call(functools.partial(assemble_kernel, slots, panels, local_ti...  5.9 us
    all_to_all x1, starting transfers between devices, per_device(): lax.all_to_all(packed, 'front', split_axis=0, concat_axis=0, tiled=True)  5.2 us
    pallas_call x1, Pallas kernels, per_device(): pl.pallas_call(functools.partial(pack_kernel, slots), out_shape=jax.Shape...  4.08 us
  transfers between devices with their start and end apart: 3, of which 1 were waited for; matrix products, arithmetic and copies ran while one was open for 1% of the time, Pallas kernels for 45%

profile of v1, /device:TPU:11, one launch (start us, length us, event | category | flops | bytes accessed | tf_op | source)
XLA Modules:
  0.0 187.2 jit_solution(7636871810075848774)
XLA Ops:
  6.5 4.1 %pack.1 = bf16[8,1808,128]{2,1,0:T(8,128)(2,1)} custom-call(s32[56]{0:T(128)} %bitcast.13, s32[56]{0:T(128)} %bitcast.14, bf16[56,128,128]{2,1,0:T(8,128)(2,1)} %bitcast.9), custom_call_target="tpu_custom_call" | custom-call | tf_op jit(solution)/shard_map/pack/pallas_call | solution.py:233
  10.6 5.2 %all-to-all-start = ((bf16[8,1808,128]{2,1,0:T(8,128)(2,1)}), bf16[8,1808,128]{2,1,0:T(8,128)(2,1)}, u32[]{:S(2)}, u32[]{:S(2)}) async-start(bf16[8,1808,128]{2,1,0:T(8,128)(2,1)} %pack.1), calls=%async_computation | async-start | bytes 7405568 | tf_op jit(solution)/shard_map/all_to_all | solution.py:241
  15.8 0.0 all-gather.2.cloned.1.call-start
  15.8 0.7 pad_add_fusion.ids_ref
  16.5 41.7 %all-to-all-done.arrived_ref = bf16[8,1808,128]{2,1,0:T(8,128)(2,1)} async-done(((bf16[8,1808,128]{2,1,0:T(8,128)(2,1)}), bf16[8,1808,128]{2,1,0:T(8,128)(2,1)}, u32[]{:S(2)}, u32[]{:S(2)}) %all-to-all-start) | async-done | bytes 3702816 | tf_op jit(solution)/shard_map/all_to_all | solution.py:241
  58.2 1.3 slice_convert_fusion
  59.5 5.9 %assemble.1 = (bf16[128,512]{1,0:T(8,128)(2,1)}, bf16[128,4608]{1,0:T(8,128)(2,1)}) custom-call(s32[2]{0:T(128)} %pad_add_fusion.ids_ref, s32[8,14]{1,0:T(8,128)} %bitcast.12, bf16[8,1808,128]{2,1,0:T(8,128)(2,1)} %all-to-all-done.arrived_ref), custom_call_target="tpu_custom_call" | custom-call | tf_op jit(solution)/shard_map/assemble/pallas_call | solution.py:244
  65.4 0.0 copy-start
  65.4 0.0 all-gather.2.cloned.1.call-update
  65.4 1.3 slice.7.fric_ref
  66.7 0.0 copy-done
  66.7 17.8 %all_gather.6.head_ref = bf16[512,512]{1,0:T(8,128)(2,1)} all-gather(bf16[128,512]{1,0:T(8,128)(2,1)S(1)} %copy-done), channel_id=1, replica_groups=mesh['front'=8,'panel'=4] {'panel'}, dimensions={0}, use_global_device_ids=true | all-gather | bytes 655360 | tf_op jit(solution)/shard_map/all_gather | solution.py:255
  84.5 79.8 %factor.1 = (bf16[384,512]{1,0:T(8,128)(2,1)}, bf16[384,512]{1,0:T(8,128)(2,1)}) custom-call(bf16[512,512]{1,0:T(8,128)(2,1)} %all_gather.6.head_ref, f32[1,512]{1,0:T(1,128)} %slice.7.fric_ref, bf16[128,4608]{1,0:T(8,128)(2,1)} %get-tuple-element.10.below_ref), custom_call_target="tpu_custom_call" | custom-call | flops 30000001024 | bytes 4000000 | tf_op jit(solution)/shard_map/factor/pallas_call | solution.py:258
  164.4 0.0 all-gather.2.cloned.1.call-done.all_ref
  164.4 5.2 %schur_other.1 = f32[384,768]{1,0:T(8,128)} custom-call(s32[2]{0:T(128)} %pad_add_fusion.ids_ref, bf16[384,512]{1,0:T(8,128)(2,1)} %get-tuple-element.11.high_ref, bf16[384,512]{1,0:T(8,128)(2,1)} %get-tuple-element.12.low_ref, bf16[128,4608]{1,0:T(8,128)(2,1)} %get-tuple-element.10.below_ref, f32[16,1,128]{2,1,0:T(1,128)} %bitcast.10, ...), custom_call_target="tpu_custom_call" | custom-call | flops 1000000000 | bytes 4000000 | tf_op jit(solution)/shard_map/schur_other/pallas_call | solution.py:272
  169.5 3.2 %collective-permute-start = (f32[384,768]{1,0:T(8,128)}, f32[384,768]{1,0:T(8,128)S(1)}, u32[]{:S(2)}, u32[]{:S(2)}) collective-permute-start(f32[384,768]{1,0:T(8,128)} %schur_other.1), channel_id=1, source_target_pairs={{0,4},{4,0},{8,12},{12,8},{16,20},{20,16},{24,28},{28,24},{1,5},{5... | collective-permute-start | bytes 3538952 | tf_op jit(solution)/shard_map/ppermute | solution.py:282
  172.7 5.2 %schur_keep.1 = f32[384,768]{1,0:T(8,128)} custom-call(s32[2]{0:T(128)} %pad_add_fusion.ids_ref, bf16[384,512]{1,0:T(8,128)(2,1)} %get-tuple-element.11.high_ref, bf16[384,512]{1,0:T(8,128)(2,1)} %get-tuple-element.12.low_ref, bf16[128,4608]{1,0:T(8,128)(2,1)} %get-tuple-element.10.below_ref, f32[16,1,128]{2,1,0:T(1,128)} %bitcast.11, ...), custom_call_target="tpu_custom_call" | custom-call | flops 1000000000 | bytes 4000000 | tf_op jit(solution)/shard_map/schur_keep/pallas_call | solution.py:272
  177.9 0.0 collective-permute-done
  177.9 2.4 %add_bitcast_fusion = f32[1,384,768]{2,1,0:T(8,128)} fusion(f32[384,768]{1,0:T(8,128)} %schur_keep.1, f32[384,768]{1,0:T(8,128)S(1)} %collective-permute-done), kind=kLoop, calls=%fused_computation | loop fusion | flops 294912 | bytes 3538944 | tf_op jit(solution)/shard_map/broadcast_in_dim | solution.py:284
Async XLA Ops:
  10.6 47.6 %all-to-all-start = ((bf16[8,1808,128]{2,1,0:T(8,128)(2,1)}), bf16[8,1808,128]{2,1,0:T(8,128)(2,1)}, u32[]{:S(2)}, u32[]{:S(2)}) async-start(bf16[8,1808,128]{2,1,0:T(8,128)(2,1)} %pack.1), calls=%async_computation | async-start | bytes 7405568 | tf_op jit(solution)/shard_map/all_to_all | solution.py:241
  15.8 148.6 %all-gather.2.cloned.1.call-start = ((), (), s32[]{:S(2)}) async-start(), calls=%async_computation.1 | async-start | bytes 5898240 | tf_op jit(solution)/shard_map/all_gather | solution.py:256
  65.4 1.3 copy-start
  169.5 8.3 %collective-permute-start = (f32[384,768]{1,0:T(8,128)}, f32[384,768]{1,0:T(8,128)S(1)}, u32[]{:S(2)}, u32[]{:S(2)}) collective-permute-start(f32[384,768]{1,0:T(8,128)} %schur_other.1), channel_id=1, source_target_pairs={{0,4},{4,0},{8,12},{12,8},{16,20},{20,16},{24,28},{28,24},{1,5},{5... | collective-permute-start | bytes 3538952 | tf_op jit(solution)/shard_map/ppermute | solution.py:282
Sparse Core Ops, SparseCore 0:
  65.6 91.3 all-gather.1

commit v2 on v1

--- a/solution.py
+++ b/solution.py
@@ -105,38 +105,72 @@
             start += (j + 1) * panels * edge
 
 
-def invert_unit(block):
+def eliminate(block):
     edge = block.shape[0]
     count = edge // 8
     sub = lax.broadcasted_iota(jnp.int32, (8, edge), 0)
     lane = lax.broadcasted_iota(jnp.int32, (8, edge), 1)
     a = [block[8 * g : 8 * g + 8] for g in range(count)]
     e = [jnp.where(lane == sub + 8 * g, 1.0, 0.0).astype(F32) for g in range(count)]
-    inv = [None] * count
-    for k in range(edge):
-        g, s = divmod(k, 8)
-        a_row = a[g][s : s + 1]
-        e_row = e[g][s : s + 1]
-        pivot = jnp.broadcast_to(a_row[:, k : k + 1], (8, edge))
-        flip = 1.0 / pivot
-        inv[g] = flip if s == 0 else jnp.where(sub >= s, flip, inv[g])
-        qa = jnp.broadcast_to(a_row, (8, edge)) * flip
-        qe = jnp.broadcast_to(e_row, (8, edge)) * flip
-        for i in range(g, count):
-            if i == g and s == 7:
-                continue
-            column = jnp.broadcast_to(a[i][:, k : k + 1], (8, edge))
-            if i == g:
-                column = jnp.where(sub > s, column, 0.0)
-            a[i] = a[i] - column * qa
-            e[i] = e[i] - column * qe
-    return jnp.concatenate(e, axis=0), jnp.concatenate(inv, axis=0)
-
-
-def factor_kernel(width, head_ref, fric_ref, below_ref, high_ref, low_ref, a_ref, e_ref, d_ref):
-    edge = below_ref.shape[0]
+    q = []
+
+    def across(x, k):
+        return jnp.broadcast_to(x[:, k : k + 1], (8, edge))
+
+    def down(x, k):
+        return jnp.broadcast_to(x[k : k + 1], (8, edge))
+
+    for g in range(count):
+        work = [across(a[g], 8 * g + s) for s in range(8)] + [a[g], e[g]]
+        for s in range(0, 8, 2):
+            u, v = work[s], work[s + 1]
+            p11, p21, p12, p22 = down(u, s), down(u, s + 1), down(v, s), down(v, s + 1)
+            flip = 1.0 / (p11 * p22 - p12 * p21)
+            p11, p21, p12, p22 = p11 * flip, p21 * flip, p12 * flip, p22 * flip
+            for t in range(s + 2, 10):
+                x = work[t]
+                x1, x2 = down(x, s), down(x, s + 1)
+                y1 = p22 * x1 - p12 * x2
+                y2 = p11 * x2 - p21 * x1
+                x = x - u * y1 - v * y2
+                work[t] = jnp.where(sub == s, y1, jnp.where(sub == s + 1, y2, x))
+        qa, qe = work[8], work[9]
+        q.append(qe)
+        if g + 1 < count:
+            ra = [down(qa, s) for s in range(8)]
+            re = [down(qe, s) for s in range(8)]
+        for i in range(g + 1, count):
+            xa, xe = a[i], e[i]
+            cols = [across(xa, 8 * g + s) for s in range(8)]
+            for s in range(8):
+                xa = xa - cols[s] * ra[s]
+                xe = xe - cols[s] * re[s]
+            a[i], e[i] = xa, xe
+    return jnp.concatenate(e, axis=0), jnp.concatenate(q, axis=0)
+
+
+def stages(first, last, edge, a_ref, e_ref, q_ref):
+    order = a_ref.shape[0]
+    below_rows = lax.broadcasted_iota(jnp.int32, (order, 1), 0)
+
+    def stage(b, carry):
+        here = pl.ds(pl.multiple_of(b * edge, edge), edge)
+        unit, ready = eliminate(a_ref[here, here])
+        up = dot3(ready, a_ref[here, :], NN)
+        ue = dot3(ready, e_ref[here, :], NN)
+        left = dot3(a_ref[:, here], unit, NT)
+        left = jnp.where(below_rows >= (b + 1) * edge, left, 0.0)
+        e_ref[here, :] = dot3(unit, e_ref[here, :], NN)
+        q_ref[here, :] = ue
+        a_ref[...] -= dot3(left, up, NN)
+        e_ref[...] -= dot3(left, ue, NN)
+        return carry
+
+    lax.fori_loop(first, last, stage, 0)
+
+
+def factor_start(width, edge, last, head_ref, fric_ref, a_ref, e_ref, q_ref):
     order = head_ref.shape[0]
-    blocks = order // edge
     head = head_ref[...]
     gram = dot(head, head, NT) * (1.0 / width)
     row = lax.broadcasted_iota(jnp.int32, (order, order), 0)
@@ -144,27 +178,20 @@
     eye = row == col
     a_ref[...] = gram + jnp.where(eye, fric_ref[...], 0.0)
     e_ref[...] = jnp.where(eye, 1.0, 0.0).astype(F32)
-    below_rows = lax.broadcasted_iota(jnp.int32, (order, 1), 0)
-
-    def stage(b, carry):
-        here = pl.ds(pl.multiple_of(b * edge, edge), edge)
-        unit, flip = invert_unit(a_ref[here, here])
-        up = dot3(unit, a_ref[here, :], NN)
-        ue = dot3(unit, e_ref[here, :], NN)
-        left = dot3(a_ref[:, here], unit, NT)
-        left = jnp.where(below_rows >= (b + 1) * edge, left, 0.0)
-        scale = jnp.concatenate([flip] * blocks, axis=1)
-        e_ref[here, :] = ue
-        d_ref[here, :] = scale
-        a_ref[...] -= dot3(left, up * scale, NN)
-        e_ref[...] -= dot3(left, ue * scale, NN)
-        return carry
-
-    lax.fori_loop(0, blocks, stage, 0)
+    stages(0, last, edge, a_ref, e_ref, q_ref)
+
+
+def factor_end(width, edge, first, head_ref, below_ref, a_in, e_in, q_in, high_ref, low_ref, a_ref, e_ref, q_ref):
+    order = head_ref.shape[0]
+    a_ref[...] = a_in[...]
+    e_ref[...] = e_in[...]
+    q_ref[...] = q_in[...]
+    stages(first, order // edge, edge, a_ref, e_ref, q_ref)
+    head = head_ref[...]
     eh, el = split(e_ref[...])
-    guess = dot(eh, head, NN) + dot(el, head, NN)
-    gh, gl = split(guess)
-    dh, dl = split(guess * (d_ref[...] * (1.0 / width)))
+    gh, gl = split(dot(eh, head, NN) + dot(el, head, NN))
+    qh, ql = split(q_ref[...])
+    dh, dl = split((dot(qh, head, NN) + dot(ql, head, NN)) * (1.0 / width))
     start = 0
     for j in range(high_ref.shape[0] // edge):
         mine = below_ref[:, start : start + order]
@@ -176,46 +203,78 @@
         low_ref[j * edge : (j + 1) * edge, :] = tl
 
 
-def schur_kernel(width, panels, flip_side, ids_ref, high_ref, low_ref, below_ref, fric_ref, all_ref, out_ref):
+def trimmed(rows, panels, hops):
+    return [(j + 1) * panels - hops for j in range(1, rows + 1)]
+
+
+def shorten(array, old, new, edge):
+    parts, start = [], 0
+    for was, now in zip(old, new):
+        parts.append(array[:, start * edge : (start + now) * edge])
+        start += was
+    return jnp.concatenate(parts, axis=1)
+
+
+def owner_block(width, panels, me, side, owner, own, counts, theirs_ref, high_ref, low_ref, below_ref, fric_ref, out_ref):
     edge = below_ref.shape[0]
     order = high_ref.shape[1]
     rows = high_ref.shape[0] // edge
     half = panels // 2
-    me = ids_ref[0]
-    side = ids_ref[1]
-    part = 1 - side if flip_side else side
-    picked = pl.ds(pl.multiple_of(part * half * edge, edge), half * edge)
     starts = [0]
     for j in range(rows):
         starts.append(starts[-1] + (j + 2) * order)
+    place = (owner // half + side) % 2
+    base = (owner % half) * (rows * edge)
     row = lax.broadcasted_iota(jnp.int32, (edge, edge), 0)
     col = lax.broadcasted_iota(jnp.int32, (edge, edge), 1)
+    first = 0
     for jc in range(rows):
-        first = starts[jc]
-        last = first + (jc + 2) * order
-        span = (jc + 1) * order
-        theirs = all_ref[picked, first : first + order]
-        rest = all_ref[picked, first + order : last]
+        cols = pl.ds(pl.multiple_of(base + jc * edge, edge), edge)
+        if jc > 0:
+            out_ref[place, : jc * edge, cols] = jnp.zeros((jc * edge, edge), F32)
+        if jc >= len(counts):
+            out_ref[place, jc * edge :, cols] = jnp.zeros(((rows - jc) * edge, edge), F32)
+            continue
+        last = first + counts[jc] * edge
+        span = counts[jc] * edge - order
         mine = jnp.concatenate(
             [below_ref[:, starts[j] + order : starts[j] + order + span] for j in range(jc, rows)], axis=0
         )
-        total = dot(mine, rest, NT)
-        total += dot(high_ref[jc * edge :, :], theirs, NT)
-        total += dot(low_ref[jc * edge :, :], theirs, NT)
+        total = dot(mine, theirs_ref[:, first + order : last], NT)
+        total += dot(high_ref[jc * edge :, :], theirs_ref[:, first : first + order], NT)
+        total += dot(low_ref[jc * edge :, :], theirs_ref[:, first : first + order], NT)
         total = total * (1.0 / width)
-        for q in range(half):
-            owner = part * half + q
-            cols = slice(q * rows * edge + jc * edge, q * rows * edge + (jc + 1) * edge)
-            for j in range(rows):
-                if j < jc:
-                    out_ref[j * edge : (j + 1) * edge, cols] = jnp.zeros((edge, edge), F32)
-                    continue
-                tile = total[(j - jc) * edge : (j - jc + 1) * edge, q * edge : (q + 1) * edge]
-                if j == jc:
-                    fric = fric_ref[(j + 1) * panels + me]
-                    tile += jnp.where((row == col) & (owner == me), fric, 0.0)
-                    tile = jnp.where(owner * edge + col <= me * edge + row, tile, 0.0)
-                out_ref[j * edge : (j + 1) * edge, cols] = tile
+        first = last
+        top = total[:edge]
+        if own:
+            top += jnp.where(row == col, fric_ref[(jc + 1) * panels + me], 0.0)
+        top = jnp.where(owner * edge + col <= me * edge + row, top, 0.0)
+        out_ref[place, jc * edge : (jc + 1) * edge, cols] = top
+        if jc + 1 < rows:
+            out_ref[place, (jc + 1) * edge :, cols] = total[edge:]
+
+
+def schur_kernel(width, panels, hops, own, aliased, ids_ref, high_ref, low_ref, below_ref, fric_ref, *rest):
+    rest = list(rest)
+    out_ref = rest.pop()
+    if aliased:
+        out_ref[...] = rest.pop()[...]
+    me = ids_ref[0]
+    side = ids_ref[1]
+    rows = high_ref.shape[0] // below_ref.shape[0]
+    run = functools.partial(owner_block, width, panels, me, side)
+    shared = (high_ref, low_ref, below_ref, fric_ref, out_ref)
+    if own:
+        run(me, True, trimmed(rows, panels, 0), below_ref, *shared)
+    for hop, up_ref, down_ref in zip(hops, rest[0::2], rest[1::2]):
+
+        @pl.when(me >= hop)
+        def _():
+            run(me - hop, False, trimmed(rows, panels, hop), up_ref, *shared)
+
+        @pl.when(me + hop < panels)
+        def _():
+            run(me + hop, False, trimmed(rows, panels, 0)[:-1], down_ref, *shared)
 
 
 def per_device(elem_tiles, targets, tile_places, friction):
@@ -253,35 +312,59 @@
         name="assemble",
     )(ids, places, arrived)
     head_rows = lax.all_gather(head, "panel", axis=0, tiled=True)
-    all_rows = lax.all_gather(below, "panel", axis=0, tiled=True)
-    rows = (local_tiles - 1) * edge
+    rows_below = local_tiles - 1
+    rows = rows_below * edge
+    fric_tiles = friction.reshape(col_tiles, 1, edge)
+    climb = [(i, i + 1) for i in range(panels - 1)]
+    sink = [(i + 1, i) for i in range(panels - 1)]
+    ups, downs = [], []
+    up, was = below, trimmed(rows_below, panels, 0)
+    down = below[:, : sum(was[:-1]) * edge]
+    for hop in range(1, panels):
+        now = trimmed(rows_below, panels, hop)
+        up = lax.ppermute(shorten(up, was, now, edge), "panel", climb)
+        down = lax.ppermute(down, "panel", sink)
+        was = now
+        ups.append(up)
+        downs.append(down)
+    square = jax.ShapeDtypeStruct((order, order), F32)
+    middle = panels // 2
+    state = pl.pallas_call(
+        functools.partial(factor_start, width, edge, middle),
+        out_shape=(square,) * 3,
+        in_specs=[VMEM, VMEM],
+        out_specs=(VMEM,) * 3,
+        cost_estimate=pl.CostEstimate(flops=15_000_000_000, bytes_accessed=4_000_000, transcendentals=0),
+        name="factor_start",
+    )(head_rows, friction[:, :order])
     high, low = pl.pallas_call(
-        functools.partial(factor_kernel, width),
-        out_shape=(
-            jax.ShapeDtypeStruct((rows, order), BF16),
-            jax.ShapeDtypeStruct((rows, order), BF16),
-        ),
-        in_specs=[VMEM, VMEM, VMEM],
+        functools.partial(factor_end, width, edge, middle),
+        out_shape=(jax.ShapeDtypeStruct((rows, order), BF16),) * 2,
+        in_specs=[VMEM] * 5,
         out_specs=(VMEM, VMEM),
         scratch_shapes=[pltpu.VMEM((order, order), F32)] * 3,
-        cost_estimate=pl.CostEstimate(flops=30_000_000_000, bytes_accessed=4_000_000, transcendentals=0),
-        name="factor",
-    )(head_rows, friction[:, :order], below)
-
-    def schur_half(flip_side):
+        cost_estimate=pl.CostEstimate(flops=15_000_000_000, bytes_accessed=4_000_000, transcendentals=0),
+        name="factor_end",
+    )(head_rows, below, *state)
+    shared = (ids, high, low, below, fric_tiles)
+    both = jax.ShapeDtypeStruct((2, rows, rows * panels // 2), F32)
+
+    def schur(hops, own, *arrays):
+        aliased = not own
         return pl.pallas_call(
-            functools.partial(schur_kernel, width, panels, flip_side),
-            out_shape=jax.ShapeDtypeStruct((rows, rows * panels // 2), F32),
-            in_specs=[SMEM, VMEM, VMEM, VMEM, VMEM, VMEM],
+            functools.partial(schur_kernel, width, panels, hops, own, aliased),
+            out_shape=both,
+            in_specs=[SMEM] + [VMEM] * (len(shared) - 1 + len(arrays)),
             out_specs=VMEM,
-            cost_estimate=pl.CostEstimate(flops=1_000_000_000, bytes_accessed=4_000_000, transcendentals=0),
-            name="schur_other" if flip_side else "schur_keep",
-        )(ids, high, low, below, friction.reshape(col_tiles, 1, edge), all_rows)
-
-    other = schur_half(True)
-    partner = lax.ppermute(other, "front", [(i, i ^ 1) for i in range(groups)])
-    keep = schur_half(False)
-    return (keep + partner)[None]
+            cost_estimate=pl.CostEstimate(flops=2_000_000_000, bytes_accessed=4_000_000, transcendentals=0),
+            name="schur_near" if own else "schur_far",
+        )(*shared, *arrays)
+
+    near = [x for pair in zip(ups[:-1], downs[:-1]) for x in pair]
+    mixed = schur(range(1, panels - 1), True, *near)
+    mixed = schur([panels - 1], False, ups[-1], downs[-1], mixed)
+    partner = lax.ppermute(mixed[1], "front", [(i, i ^ 1) for i in range(groups)])
+    return (mixed[0] + partner)[None]
 
 
 def solution(mesh):

time: 189 us -> 169 us (0.89)
  Pallas kernels: 100 us -> 55.4 us
  starting transfers between devices: 8.36 us -> 28.3 us
  between operations: 13.4 us -> 0.22 us
  blocking collectives: 17.8 us -> 28.7 us
  local copies, waits for them, and re-layouts: 1.31 us -> 6.92 us
  waiting for transfers between devices: 41.7 us -> 44.2 us
    pallas_call x3 -> x4, Pallas kernels: 90.2 us -> 45.7 us  [the longest x1 18.9 us: per_device(): pl.pallas_call(functools.partial(factor_end, width, edge, middle), out_sh...]
    ppermute x1 -> x7, starting transfers between devices: 3.16 us -> 23.1 us  [the longest x3 9.11 us: per_device(): down = lax.ppermute(down, 'panel', sink)]
    all_gather x1, blocking collectives: 17.8 us -> 28.7 us  [per_device(): head_rows = lax.all_gather(head, 'panel', axis=0, tiled=True)]
    ppermute x1 -> x7, waiting for transfers between devices: 0.01 us -> 2.49 us  [the longest x1 2.47 us: per_device(): lax.ppermute(mixed[1], 'front', [(i, i ^ 1) for i in range(groups)])]
    slice x0 -> x10, local copies, waits for them, and re-layouts: none -> 2.38 us  [the longest x9 2.34 us: shorten(): parts.append(array[:, start * edge:(start + now) * edge])]
  transfers between devices with their start and end apart: 3 -> 8, of which waited for: 1 -> 2; matrix products, arithmetic and copies ran while one was open for 1% -> 1% of each run, Pallas kernels for 45% -> 25%
where the time goes in v2:
time: 169 us; the launch traced here: 167 us
  Pallas kernels  55.4 us (33%)
  waiting for transfers between devices  44.2 us (26%)
  blocking collectives  28.7 us (17%)
  starting transfers between devices  28.3 us (17%)
  local copies, waits for them, and re-layouts  6.92 us (4%)
  other arithmetic  3.33 us (2%)
    all_to_all x1, waiting for transfers between devices, per_device(): lax.all_to_all(packed, 'front', split_axis=0, concat_axis=0, tiled=True)  41.7 us
    all_gather x1, blocking collectives, per_device(): head_rows = lax.all_gather(head, 'panel', axis=0, tiled=True)  28.7 us
    pallas_call x1, Pallas kernels, per_device(): pl.pallas_call(functools.partial(factor_end, width, edge, middle), out_sh...  18.9 us
    pallas_call x1, Pallas kernels, per_device(): pl.pallas_call(functools.partial(factor_start, width, edge, middle), out_...  15.1 us
    pallas_call x2, Pallas kernels, schur(): pl.pallas_call(functools.partial(schur_kernel, width, panels, hops, own,...  11.6 us
    ppermute x3, starting transfers between devices, per_device(): down = lax.ppermute(down, 'panel', sink)  9.11 us
    ppermute x3, starting transfers between devices, per_device(): up = lax.ppermute(shorten(up, was, now, edge), 'panel', climb)  7.48 us
    ppermute x1, starting transfers between devices, per_device(): lax.ppermute(mixed[1], 'front', [(i, i ^ 1) for i in range(groups)])  6.47 us
  transfers between devices with their start and end apart: 8, of which 2 were waited for; matrix products, arithmetic and copies ran while one was open for 1% of the time, Pallas kernels for 25%

profile of v2, /device:TPU:11, one launch (start us, length us, event | category | flops | bytes accessed | tf_op | source)
XLA Modules:
  0.0 167.0 jit_solution(8802272485669715064)
XLA Ops:
  0.0 4.1 %pack.1 = bf16[8,1808,128]{2,1,0:T(8,128)(2,1)} custom-call(s32[56]{0:T(128)} %bitcast.21, s32[56]{0:T(128)} %bitcast.22, bf16[56,128,128]{2,1,0:T(8,128)(2,1)} %bitcast.17), custom_call_target="tpu_custom_call" | custom-call | tf_op jit(solution)/shard_map/pack/pallas_call | solution.py:292
  4.1 5.2 %all-to-all-start = ((bf16[8,1808,128]{2,1,0:T(8,128)(2,1)}), bf16[8,1808,128]{2,1,0:T(8,128)(2,1)}, u32[]{:S(2)}, u32[]{:S(2)}) async-start(bf16[8,1808,128]{2,1,0:T(8,128)(2,1)} %pack.1), calls=%async_computation | async-start | bytes 7405568 | tf_op jit(solution)/shard_map/all_to_all | solution.py:300
  9.3 0.7 pad_add_fusion.ids_ref
  10.0 41.7 %all-to-all-done.arrived_ref = bf16[8,1808,128]{2,1,0:T(8,128)(2,1)} async-done(((bf16[8,1808,128]{2,1,0:T(8,128)(2,1)}), bf16[8,1808,128]{2,1,0:T(8,128)(2,1)}, u32[]{:S(2)}, u32[]{:S(2)}) %all-to-all-start) | async-done | bytes 3702816 | tf_op jit(solution)/shard_map/all_to_all | solution.py:300
  51.7 1.3 slice_convert_fusion
  53.0 5.7 %assemble.1 = (bf16[128,512]{1,0:T(8,128)(2,1)}, bf16[128,4608]{1,0:T(8,128)(2,1)}) custom-call(s32[2]{0:T(128)} %pad_add_fusion.ids_ref, s32[8,14]{1,0:T(8,128)} %bitcast.20, bf16[8,1808,128]{2,1,0:T(8,128)(2,1)} %all-to-all-done.arrived_ref), custom_call_target="tpu_custom_call" | custom-call | tf_op jit(solution)/shard_map/assemble/pallas_call | solution.py:303
  58.6 0.0 copy-start
  58.6 1.2 slice.46
  59.8 1.0 slice.45
  60.8 0.0 copy-done
  60.9 0.0 copy-start.5
  60.9 0.1 pad_maximum_fusion
  61.0 3.2 %collective-permute-start = (bf16[128,4224]{1,0:T(8,128)(2,1)S(1)}, bf16[128,4224]{1,0:T(8,128)(2,1)S(1)}, u32[]{:S(2)}, u32[]{:S(2)}) collective-permute-start(bf16[128,4224]{1,0:T(8,128)(2,1)S(1)} %pad_maximum_fusion), channel_id=1, source_target_pairs={{0,1},{1,2},{2,3},{4,5},{5,6},{6,7},{8,9},{9,10},{10,11},{12,13},{... | collective-permute-start | bytes 3244040 | tf_op jit(solution)/shard_map/ppermute | solution.py:325
  64.2 2.1 %collective-permute-start.3 = (bf16[128,2560]{1,0:T(8,128)(2,1)S(1)}, bf16[128,2560]{1,0:T(8,128)(2,1)}, u32[]{:S(2)}, u32[]{:S(2)}) collective-permute-start(bf16[128,2560]{1,0:T(8,128)(2,1)S(1)} %slice.53), channel_id=1, source_target_pairs={{1,0},{2,1},{3,2},{5,4},{6,5},{7,6},{9,8},{10,9},{11,10},{13,12},{... | collective-permute-start | bytes 1966088 | tf_op jit(solution)/shard_map/ppermute | solution.py:326
  66.4 1.3 slice.43.fric_ref
  67.7 0.0 copy-done.5
  67.7 28.7 %all_gather.3.head_ref = bf16[512,512]{1,0:T(8,128)(2,1)} all-gather(bf16[128,512]{1,0:T(8,128)(2,1)S(1)} %copy-done.5), channel_id=1, replica_groups=mesh['front'=8,'panel'=4] {'panel'}, dimensions={0}, use_global_device_ids=true | all-gather | bytes 655360 | tf_op jit(solution)/shard_map/all_gather | solution.py:314
  96.3 0.0 collective-permute-done.3.rest_1_
  96.3 3.6 %collective-permute-start.4 = (bf16[128,2560]{1,0:T(8,128)(2,1)}, bf16[128,2560]{1,0:T(8,128)(2,1)}, u32[]{:S(2)}, u32[]{:S(2)}) collective-permute-start(bf16[128,2560]{1,0:T(8,128)(2,1)} %collective-permute-done.3.rest_1_), channel_id=1, source_target_pairs={{1,0},{2,1},{3,2},{5,4},{6,5},{7,6},{9,8},{10,9},{11,10},{13,12},{... | collective-permute-start | bytes 1966088 | tf_op jit(solution)/shard_map/ppermute | solution.py:326
  99.9 0.0 collective-permute-done.rest_0_
  100.0 0.0 copy-start.2
  100.1 0.1 pad_maximum_fusion.1
  100.1 0.8 copy-done.2
  101.0 1.9 %collective-permute-start.1 = (bf16[128,3840]{1,0:T(8,128)(2,1)S(1)}, bf16[128,3840]{1,0:T(8,128)(2,1)S(1)}, u32[]{:S(2)}, u32[]{:S(2)}) collective-permute-start(bf16[128,3840]{1,0:T(8,128)(2,1)S(1)} %pad_maximum_fusion.1), channel_id=1, source_target_pairs={{0,1},{1,2},{2,3},{4,5},{5,6},{6,7},{8,9},{9,10},{10,11},{12,13},{... | collective-permute-start | bytes 2949128 | tf_op jit(solution)/shard_map/ppermute | solution.py:325
  102.9 15.1 %factor_start.1 = (f32[512,512]{1,0:T(8,128)}, f32[512,512]{1,0:T(8,128)}, f32[512,512]{1,0:T(8,128)}) custom-call(bf16[512,512]{1,0:T(8,128)(2,1)} %all_gather.3.head_ref, f32[1,512]{1,0:T(1,128)} %slice.43.fric_ref), custom_call_target="tpu_custom_call" | custom-call | flops 15000000512 | bytes 4000000 | tf_op jit(solution)/shard_map/factor_start/pallas_call | solution.py:332
  118.0 0.0 collective-permute-done.4.rest_3_
  118.0 3.4 %collective-permute-start.5 = (bf16[128,2560]{1,0:T(8,128)(2,1)}, bf16[128,2560]{1,0:T(8,128)(2,1)}, u32[]{:S(2)}, u32[]{:S(2)}) collective-permute-start(bf16[128,2560]{1,0:T(8,128)(2,1)} %collective-permute-done.4.rest_3_), channel_id=1, source_target_pairs={{1,0},{2,1},{3,2},{5,4},{6,5},{7,6},{9,8},{10,9},{11,10},{13,12},{... | collective-permute-start | bytes 1966088 | tf_op jit(solution)/shard_map/ppermute | solution.py:326
  121.4 0.0 collective-permute-done.1.rest_2_
  121.4 0.0 copy-start.3
  121.5 0.1 pad_maximum_fusion.2
  121.5 2.3 %collective-permute-start.2 = (bf16[128,3456]{1,0:T(8,128)(2,1)S(1)}, bf16[128,3456]{1,0:T(8,128)(2,1)S(1)}, u32[]{:S(2)}, u32[]{:S(2)}) collective-permute-start(bf16[128,3456]{1,0:T(8,128)(2,1)S(1)} %pad_maximum_fusion.2), channel_id=1, source_target_pairs={{0,1},{1,2},{2,3},{4,5},{5,6},{6,7},{8,9},{9,10},{10,11},{12,13},{... | collective-permute-start | bytes 2654216 | tf_op jit(solution)/shard_map/ppermute | solution.py:325
  123.9 0.0 copy-done.3
  123.9 18.9 %factor_end.1 = (bf16[384,512]{1,0:T(8,128)(2,1)}, bf16[384,512]{1,0:T(8,128)(2,1)}) custom-call(bf16[512,512]{1,0:T(8,128)(2,1)} %all_gather.3.head_ref, bf16[128,4608]{1,0:T(8,128)(2,1)} %get-tuple-element.13.below_ref, f32[512,512]{1,0:T(8,128)} %get-tuple-element.14.a_in, f32[512,512]{1,0:T(8,128)} %get-tuple-element.15.e_in, ...), custom_call_target="tpu_custom_call" | custom-call | flops 15000000512 | bytes 4000000 | tf_op jit(solution)/shard_map/factor_end/pallas_call | solution.py:340
  142.9 7.3 %schur_near.1.rest_2_ = f32[2,384,768]{2,1,0:T(8,128)} custom-call(s32[2]{0:T(128)} %pad_add_fusion.ids_ref, bf16[384,512]{1,0:T(8,128)(2,1)} %get-tuple-element.17.high_ref, bf16[384,512]{1,0:T(8,128)(2,1)} %get-tuple-element.18.low_ref, bf16[128,4608]{1,0:T(8,128)(2,1)} %get-tuple-element.13.below_ref, f32[16,1,128]{2,1,0:T(1,128)} %bitcast.18, ...), custom_call_target="tpu_custom_call" | custom-call | flops 2000000000 | bytes 4000000 | tf_op jit(solution)/shard_map/schur_near/pallas_call | solution.py:354
  150.2 0.0 collective-permute-done.5.rest_1_
  150.2 0.0 collective-permute-done.2.rest_0_
  150.2 0.0 copy-start.4
  150.2 0.9 copy-done.4
  151.1 4.3 %schur_far.1 = f32[2,384,768]{2,1,0:T(8,128)} custom-call(s32[2]{0:T(128)} %pad_add_fusion.ids_ref, bf16[384,512]{1,0:T(8,128)(2,1)} %get-tuple-element.17.high_ref, bf16[384,512]{1,0:T(8,128)(2,1)} %get-tuple-element.18.low_ref, bf16[128,4608]{1,0:T(8,128)(2,1)} %get-tuple-element.13.below_ref, f32[16,1,128]{2,1,0:T(1,128)} %bitcast.19, ...), custom_call_target="tpu_custom_call" | custom-call | flops 2000000000 | bytes 4000000 | tf_op jit(solution)/shard_map/schur_far/pallas_call | solution.py:354
  155.4 0.0 copy-start.1
  155.4 1.5 slice_bitcast_fusion
  156.9 6.5 %collective-permute-start.6 = (f32[384,768]{1,0:T(8,128)S(1)}, f32[384,768]{1,0:T(8,128)S(1)}, u32[]{:S(2)}, u32[]{:S(2)}) collective-permute-start(f32[384,768]{1,0:T(8,128)S(1)} %slice_bitcast_fusion), channel_id=1, source_target_pairs={{0,4},{4,0},{8,12},{12,8},{16,20},{20,16},{24,28},{28,24},{1,5},{5... | collective-permute-start | bytes 3538952 | tf_op jit(solution)/shard_map/ppermute | solution.py:366
  163.4 2.5 %collective-permute-done.6 = f32[384,768]{1,0:T(8,128)S(1)} collective-permute-done((f32[384,768]{1,0:T(8,128)S(1)}, f32[384,768]{1,0:T(8,128)S(1)}, u32[]{:S(2)}, u32[]{:S(2)}) %collective-permute-start.6) | collective-permute-done | bytes 1179680 | tf_op jit(solution)/shard_map/ppermute | solution.py:366
  165.9 0.0 copy-done.1
  165.9 1.1 fusion.1
  (8 shorter events, 0.2 us)
Async XLA Ops:
  4.1 47.6 %all-to-all-start = ((bf16[8,1808,128]{2,1,0:T(8,128)(2,1)}), bf16[8,1808,128]{2,1,0:T(8,128)(2,1)}, u32[]{:S(2)}, u32[]{:S(2)}) async-start(bf16[8,1808,128]{2,1,0:T(8,128)(2,1)} %pack.1), calls=%async_computation | async-start | bytes 7405568 | tf_op jit(solution)/shard_map/all_to_all | solution.py:300
  58.6 2.2 %copy-start = (bf16[128,4608]{1,0:T(8,128)(2,1)S(1)}, bf16[128,4608]{1,0:T(8,128)(2,1)}, u32[]{:S(2)}) copy-start(bf16[128,4608]{1,0:T(8,128)(2,1)} %get-tuple-element.13.below_ref) | copy-start | bytes 3538948
  60.9 6.8 %copy-start.5 = (bf16[128,512]{1,0:T(8,128)(2,1)S(1)}, bf16[128,512]{1,0:T(8,128)(2,1)}, u32[]{:S(2)}) copy-start(bf16[128,512]{1,0:T(8,128)(2,1)} %get-tuple-element.12) | copy-start | bytes 393220
  61.0 39.0 %collective-permute-start = (bf16[128,4224]{1,0:T(8,128)(2,1)S(1)}, bf16[128,4224]{1,0:T(8,128)(2,1)S(1)}, u32[]{:S(2)}, u32[]{:S(2)}) collective-permute-start(bf16[128,4224]{1,0:T(8,128)(2,1)S(1)} %pad_maximum_fusion), channel_id=1, source_target_pairs={{0,1},{1,2},{2,3},{4,5},{5,6},{6,7},{8,9},{9,10},{10,11},{12,13},{... | collective-permute-start | bytes 3244040 | tf_op jit(solution)/shard_map/ppermute | solution.py:325
  64.2 32.1 %collective-permute-start.3 = (bf16[128,2560]{1,0:T(8,128)(2,1)S(1)}, bf16[128,2560]{1,0:T(8,128)(2,1)}, u32[]{:S(2)}, u32[]{:S(2)}) collective-permute-start(bf16[128,2560]{1,0:T(8,128)(2,1)S(1)} %slice.53), channel_id=1, source_target_pairs={{1,0},{2,1},{3,2},{5,4},{6,5},{7,6},{9,8},{10,9},{11,10},{13,12},{... | collective-permute-start | bytes 1966088 | tf_op jit(solution)/shard_map/ppermute | solution.py:326
  96.3 21.6 %collective-permute-start.4 = (bf16[128,2560]{1,0:T(8,128)(2,1)}, bf16[128,2560]{1,0:T(8,128)(2,1)}, u32[]{:S(2)}, u32[]{:S(2)}) collective-permute-start(bf16[128,2560]{1,0:T(8,128)(2,1)} %collective-permute-done.3.rest_1_), channel_id=1, source_target_pairs={{1,0},{2,1},{3,2},{5,4},{6,5},{7,6},{9,8},{10,9},{11,10},{13,12},{... | collective-permute-start | bytes 1966088 | tf_op jit(solution)/shard_map/ppermute | solution.py:326
  100.0 1.0 copy-start.2
  101.0 20.4 %collective-permute-start.1 = (bf16[128,3840]{1,0:T(8,128)(2,1)S(1)}, bf16[128,3840]{1,0:T(8,128)(2,1)S(1)}, u32[]{:S(2)}, u32[]{:S(2)}) collective-permute-start(bf16[128,3840]{1,0:T(8,128)(2,1)S(1)} %pad_maximum_fusion.1), channel_id=1, source_target_pairs={{0,1},{1,2},{2,3},{4,5},{5,6},{6,7},{8,9},{9,10},{10,11},{12,13},{... | collective-permute-start | bytes 2949128 | tf_op jit(solution)/shard_map/ppermute | solution.py:325
  118.0 32.2 %collective-permute-start.5 = (bf16[128,2560]{1,0:T(8,128)(2,1)}, bf16[128,2560]{1,0:T(8,128)(2,1)}, u32[]{:S(2)}, u32[]{:S(2)}) collective-permute-start(bf16[128,2560]{1,0:T(8,128)(2,1)} %collective-permute-done.4.rest_3_), channel_id=1, source_target_pairs={{1,0},{2,1},{3,2},{5,4},{6,5},{7,6},{9,8},{10,9},{11,10},{13,12},{... | collective-permute-start | bytes 1966088 | tf_op jit(solution)/shard_map/ppermute | solution.py:326
  121.4 2.5 %copy-start.3 = (bf16[128,3840]{1,0:T(8,128)(2,1)}, bf16[128,3840]{1,0:T(8,128)(2,1)S(1)}, u32[]{:S(2)}) copy-start(bf16[128,3840]{1,0:T(8,128)(2,1)S(1)} %collective-permute-done.1.rest_2_) | copy-start | bytes 2949124
  121.5 28.6 %collective-permute-start.2 = (bf16[128,3456]{1,0:T(8,128)(2,1)S(1)}, bf16[128,3456]{1,0:T(8,128)(2,1)S(1)}, u32[]{:S(2)}, u32[]{:S(2)}) collective-permute-start(bf16[128,3456]{1,0:T(8,128)(2,1)S(1)} %pad_maximum_fusion.2), channel_id=1, source_target_pairs={{0,1},{1,2},{2,3},{4,5},{5,6},{6,7},{8,9},{9,10},{10,11},{12,13},{... | collective-permute-start | bytes 2654216 | tf_op jit(solution)/shard_map/ppermute | solution.py:325
  150.2 0.9 copy-start.4
  155.4 10.4 %copy-start.1 = (f32[2,384,768]{2,1,0:T(8,128)S(1)}, f32[2,384,768]{2,1,0:T(8,128)}, u32[]{:S(2)}) copy-start(f32[2,384,768]{2,1,0:T(8,128)} %schur_far.1) | copy-start | bytes 7077892
  156.9 8.9 %collective-permute-start.6 = (f32[384,768]{1,0:T(8,128)S(1)}, f32[384,768]{1,0:T(8,128)S(1)}, u32[]{:S(2)}, u32[]{:S(2)}) collective-permute-start(f32[384,768]{1,0:T(8,128)S(1)} %slice_bitcast_fusion), channel_id=1, source_target_pairs={{0,4},{4,0},{8,12},{12,8},{16,20},{20,16},{24,28},{28,24},{1,5},{5... | collective-permute-start | bytes 3538952 | tf_op jit(solution)/shard_map/ppermute | solution.py:366

commit v3 on v2

--- a/solution.py
+++ b/solution.py
@@ -176,7 +176,7 @@
     row = lax.broadcasted_iota(jnp.int32, (order, order), 0)
     col = lax.broadcasted_iota(jnp.int32, (order, order), 1)
     eye = row == col
-    a_ref[...] = gram + jnp.where(eye, fric_ref[...], 0.0)
+    a_ref[...] = gram + jnp.where(eye, fric_ref[:, :order], 0.0)
     e_ref[...] = jnp.where(eye, 1.0, 0.0).astype(F32)
     stages(0, last, edge, a_ref, e_ref, q_ref)
 
@@ -207,12 +207,14 @@
     return [(j + 1) * panels - hops for j in range(1, rows + 1)]
 
 
-def shorten(array, old, new, edge):
-    parts, start = [], 0
-    for was, now in zip(old, new):
-        parts.append(array[:, start * edge : (start + now) * edge])
-        start += was
-    return jnp.concatenate(parts, axis=1)
+def trim_kernel(was, now, after_ref, climbing_ref, sinking_ref, up_ref, down_ref):
+    edge = climbing_ref.shape[0]
+    start = done = 0
+    for before, after in zip(was, now):
+        up_ref[:, done * edge : (done + after) * edge] = climbing_ref[:, start * edge : (start + after) * edge]
+        start += before
+        done += after
+    down_ref[...] = sinking_ref[:, : down_ref.shape[1]]
 
 
 def owner_block(width, panels, me, side, owner, own, counts, theirs_ref, high_ref, low_ref, below_ref, fric_ref, out_ref):
@@ -254,11 +256,12 @@
             out_ref[place, (jc + 1) * edge :, cols] = total[edge:]
 
 
-def schur_kernel(width, panels, hops, own, aliased, ids_ref, high_ref, low_ref, below_ref, fric_ref, *rest):
+def schur_kernel(width, panels, hops, own, last_call, ids_ref, high_ref, low_ref, below_ref, fric_ref, *rest):
     rest = list(rest)
     out_ref = rest.pop()
-    if aliased:
-        out_ref[...] = rest.pop()[...]
+    if last_call:
+        other_ref, keep_ref, mixed_ref = rest.pop(), rest.pop(), rest.pop()
+        out_ref[...] = mixed_ref[...]
     me = ids_ref[0]
     side = ids_ref[1]
     rows = high_ref.shape[0] // below_ref.shape[0]
@@ -275,6 +278,10 @@
         @pl.when(me + hop < panels)
         def _():
             run(me + hop, False, trimmed(rows, panels, 0)[:-1], down_ref, *shared)
+
+    if last_call:
+        keep_ref[...] = out_ref[0]
+        other_ref[...] = out_ref[1]
 
 
 def per_device(elem_tiles, targets, tile_places, friction):
@@ -318,15 +325,23 @@
     climb = [(i, i + 1) for i in range(panels - 1)]
     sink = [(i + 1, i) for i in range(panels - 1)]
     ups, downs = [], []
-    up, was = below, trimmed(rows_below, panels, 0)
-    down = below[:, : sum(was[:-1]) * edge]
-    for hop in range(1, panels):
-        now = trimmed(rows_below, panels, hop)
-        up = lax.ppermute(shorten(up, was, now, edge), "panel", climb)
-        down = lax.ppermute(down, "panel", sink)
-        was = now
-        ups.append(up)
-        downs.append(down)
+    widths = [trimmed(rows_below, panels, hop) for hop in range(panels)]
+
+    def travel(hop, after, climbing, sinking):
+        up, down = pl.pallas_call(
+            functools.partial(trim_kernel, widths[hop - 1], widths[hop]),
+            out_shape=(
+                jax.ShapeDtypeStruct((edge, sum(widths[hop]) * edge), BF16),
+                jax.ShapeDtypeStruct((edge, sum(widths[0][:-1]) * edge), BF16),
+            ),
+            in_specs=[pl.BlockSpec(memory_space=pl.ANY), VMEM, VMEM],
+            out_specs=(VMEM, VMEM),
+            name="trim",
+        )(after, climbing, sinking)
+        ups.append(lax.ppermute(up, "panel", climb))
+        downs.append(lax.ppermute(down, "panel", sink))
+
+    travel(1, head_rows, below, below)
     square = jax.ShapeDtypeStruct((order, order), F32)
     middle = panels // 2
     state = pl.pallas_call(
@@ -336,7 +351,10 @@
         out_specs=(VMEM,) * 3,
         cost_estimate=pl.CostEstimate(flops=15_000_000_000, bytes_accessed=4_000_000, transcendentals=0),
         name="factor_start",
-    )(head_rows, friction[:, :order])
+    )(head_rows, friction)
+    middle_hop = (panels + 1) // 2
+    for hop in range(2, middle_hop + 1):
+        travel(hop, state[0], ups[-1], downs[-1])
     high, low = pl.pallas_call(
         functools.partial(factor_end, width, edge, middle),
         out_shape=(jax.ShapeDtypeStruct((rows, order), BF16),) * 2,
@@ -346,25 +364,29 @@
         cost_estimate=pl.CostEstimate(flops=15_000_000_000, bytes_accessed=4_000_000, transcendentals=0),
         name="factor_end",
     )(head_rows, below, *state)
+    for hop in range(middle_hop + 1, panels):
+        travel(hop, high, ups[-1], downs[-1])
     shared = (ids, high, low, below, fric_tiles)
     both = jax.ShapeDtypeStruct((2, rows, rows * panels // 2), F32)
+    half = jax.ShapeDtypeStruct(both.shape[1:], F32)
 
     def schur(hops, own, *arrays):
-        aliased = not own
+        last_call = not own
         return pl.pallas_call(
-            functools.partial(schur_kernel, width, panels, hops, own, aliased),
-            out_shape=both,
+            functools.partial(schur_kernel, width, panels, hops, own, last_call),
+            out_shape=(half, half) if last_call else both,
             in_specs=[SMEM] + [VMEM] * (len(shared) - 1 + len(arrays)),
-            out_specs=VMEM,
+            out_specs=(VMEM, VMEM) if last_call else VMEM,
+            scratch_shapes=[pltpu.VMEM(both.shape, F32)] if last_call else [],
             cost_estimate=pl.CostEstimate(flops=2_000_000_000, bytes_accessed=4_000_000, transcendentals=0),
             name="schur_near" if own else "schur_far",
         )(*shared, *arrays)
 
     near = [x for pair in zip(ups[:-1], downs[:-1]) for x in pair]
     mixed = schur(range(1, panels - 1), True, *near)
-    mixed = schur([panels - 1], False, ups[-1], downs[-1], mixed)
-    partner = lax.ppermute(mixed[1], "front", [(i, i ^ 1) for i in range(groups)])
-    return (mixed[0] + partner)[None]
+    keep, other = schur([panels - 1], False, ups[-1], downs[-1], mixed)
+    partner = lax.ppermute(other, "front", [(i, i ^ 1) for i in range(groups)])
+    return (keep + partner)[None]
 
 
 def solution(mesh):

time: 169 us -> 171 us (1.012)
  blocking collectives: 28.7 us -> 13.3 us
  waiting for transfers between devices: 44.2 us -> 56.5 us
  Pallas kernels: 55.4 us -> 63.7 us
  local copies, waits for them, and re-layouts: 6.92 us -> 3.08 us
    all_gather x1, blocking collectives: 28.7 us -> 13.3 us  [per_device(): head_rows = lax.all_gather(head, 'panel', axis=0, tiled=True)]
    ppermute x7, waiting for transfers between devices: 2.49 us -> 14.7 us  [the longest x3 9.87 us: travel(): ups.append(lax.ppermute(up, 'panel', climb))]
    pallas_call x0 -> x3, Pallas kernels: none -> 8.24 us  [travel(): pl.pallas_call(functools.partial(trim_kernel, widths[hop - 1], widths[hop...]
    slice x11 -> x0, local copies, waits for them, and re-layouts: 3.66 us -> none  [the longest x9 2.34 us: shorten(): parts.append(array[:, start * edge:(start + now) * edge])]
  transfers between devices with their start and end apart: 8 -> 8, of which waited for: 2 -> 5; matrix products, arithmetic and copies ran while one was open for 1% -> 0% of each run, Pallas kernels for 25% -> 24%
where the time goes in v3:
time: 171 us; the launch traced here: 169 us
  Pallas kernels  63.7 us (37%)
  waiting for transfers between devices  56.5 us (33%)
  starting transfers between devices  27.7 us (16%)
  blocking collectives  13.3 us (8%)
  other arithmetic  4.36 us (3%)
  local copies, waits for them, and re-layouts  3.08 us (2%)
    all_to_all x1, waiting for transfers between devices, per_device(): lax.all_to_all(packed, 'front', split_axis=0, concat_axis=0, tiled=True)  41.8 us
    pallas_call x1, Pallas kernels, per_device(): pl.pallas_call(functools.partial(factor_end, width, edge, middle), out_sh...  18.9 us
    pallas_call x1, Pallas kernels, per_device(): pl.pallas_call(functools.partial(factor_start, width, edge, middle), out_...  15.1 us
    all_gather x1, blocking collectives, per_device(): head_rows = lax.all_gather(head, 'panel', axis=0, tiled=True)  13.3 us
    pallas_call x2, Pallas kernels, schur(): pl.pallas_call(functools.partial(schur_kernel, width, panels, hops, own,...  11.7 us
    ppermute x3, waiting for transfers between devices, travel(): ups.append(lax.ppermute(up, 'panel', climb))  9.87 us
    ppermute x3, starting transfers between devices, travel(): downs.append(lax.ppermute(down, 'panel', sink))  8.97 us
    pallas_call x3, Pallas kernels, travel(): pl.pallas_call(functools.partial(trim_kernel, widths[hop - 1], widths[hop...  8.24 us
  transfers between devices with their start and end apart: 8, of which 5 were waited for; matrix products, arithmetic and copies ran while one was open for 0% of the time, Pallas kernels for 24%

profile of v3, /device:TPU:11, one launch (start us, length us, event | category | flops | bytes accessed | tf_op | source)
XLA Modules:
  0.0 168.8 jit_solution(15985674617302905345)
XLA Ops:
  0.0 4.1 %pack.1 = bf16[8,1808,128]{2,1,0:T(8,128)(2,1)} custom-call(s32[56]{0:T(128)} %bitcast.13, s32[56]{0:T(128)} %bitcast.14, bf16[56,128,128]{2,1,0:T(8,128)(2,1)} %bitcast.9), custom_call_target="tpu_custom_call" | custom-call | tf_op jit(solution)/shard_map/pack/pallas_call | solution.py:299
  4.1 5.2 %all-to-all-start = ((bf16[8,1808,128]{2,1,0:T(8,128)(2,1)}), bf16[8,1808,128]{2,1,0:T(8,128)(2,1)}, u32[]{:S(2)}, u32[]{:S(2)}) async-start(bf16[8,1808,128]{2,1,0:T(8,128)(2,1)} %pack.1), calls=%async_computation | async-start | bytes 7405568 | tf_op jit(solution)/shard_map/all_to_all | solution.py:307
  9.3 0.6 pad_add_fusion.ids_ref
  9.9 41.8 %all-to-all-done.arrived_ref = bf16[8,1808,128]{2,1,0:T(8,128)(2,1)} async-done(((bf16[8,1808,128]{2,1,0:T(8,128)(2,1)}), bf16[8,1808,128]{2,1,0:T(8,128)(2,1)}, u32[]{:S(2)}, u32[]{:S(2)}) %all-to-all-start) | async-done | bytes 3702816 | tf_op jit(solution)/shard_map/all_to_all | solution.py:307
  51.6 1.3 slice_convert_fusion
  53.0 5.7 %assemble.1 = (bf16[128,512]{1,0:T(8,128)(2,1)}, bf16[128,4608]{1,0:T(8,128)(2,1)}) custom-call(s32[2]{0:T(128)} %pad_add_fusion.ids_ref, s32[8,14]{1,0:T(8,128)} %bitcast.10, bf16[8,1808,128]{2,1,0:T(8,128)(2,1)} %all-to-all-done.arrived_ref), custom_call_target="tpu_custom_call" | custom-call | tf_op jit(solution)/shard_map/assemble/pallas_call | solution.py:310
  58.6 13.3 %all_gather.3.head_ref.after_ref = bf16[512,512]{1,0:T(8,128)(2,1)} all-gather(bf16[128,512]{1,0:T(8,128)(2,1)} %get-tuple-element.20), channel_id=1, replica_groups=mesh['front'=8,'panel'=4] {'panel'}, dimensions={0}, use_global_device_ids=true | all-gather | bytes 655360 | tf_op jit(solution)/shard_map/all_gather | solution.py:321
  72.0 3.0 %trim.3 = (bf16[128,4224]{1,0:T(8,128)(2,1)}, bf16[128,2560]{1,0:T(8,128)(2,1)}) custom-call(bf16[512,512]{1,0:T(8,128)(2,1)} %all_gather.3.head_ref.after_ref, bf16[128,4608]{1,0:T(8,128)(2,1)} %get-tuple-element.21.below_ref.climbing_ref.sinking_ref, bf16[128,4608]{1,0:T(8,128)(2,1)} %get-tuple-element.21.below_ref.climbing_ref.sinking_ref), custom_call_target="tpu_custom_call" | custom-call | tf_op jit(solution)/shard_map/trim/pallas_call | solution.py:331
  75.0 3.7 %collective-permute-start.1 = (bf16[128,2560]{1,0:T(8,128)(2,1)}, bf16[128,2560]{1,0:T(8,128)(2,1)S(1)}, u32[]{:S(2)}, u32[]{:S(2)}) collective-permute-start(bf16[128,2560]{1,0:T(8,128)(2,1)} %get-tuple-element.28), channel_id=1, source_target_pairs={{1,0},{2,1},{3,2},{5,4},{6,5},{7,6},{9,8},{10,9},{11,10},{13,12},{... | collective-permute-start | bytes 1966088 | tf_op jit(solution)/shard_map/ppermute | solution.py:342
  78.7 1.9 %collective-permute-start = (bf16[128,4224]{1,0:T(8,128)(2,1)}, bf16[128,4224]{1,0:T(8,128)(2,1)S(1)}, u32[]{:S(2)}, u32[]{:S(2)}) collective-permute-start(bf16[128,4224]{1,0:T(8,128)(2,1)} %get-tuple-element.27), channel_id=1, source_target_pairs={{0,1},{1,2},{2,3},{4,5},{5,6},{6,7},{8,9},{9,10},{10,11},{12,13},{... | collective-permute-start | bytes 3244040 | tf_op jit(solution)/shard_map/ppermute | solution.py:341
  80.7 15.1 %factor_start.1 = (f32[512,512]{1,0:T(8,128)}, f32[512,512]{1,0:T(8,128)}, f32[512,512]{1,0:T(8,128)}) custom-call(bf16[512,512]{1,0:T(8,128)(2,1)} %all_gather.3.head_ref.after_ref, f32[1,2048]{1,0:T(1,128)} %fric_ref.1), custom_call_target="tpu_custom_call" | custom-call | flops 15000000512 | bytes 4000000 | tf_op jit(solution)/shard_map/factor_start/pallas_call | solution.py:347
  95.7 0.0 collective-permute-done.1.sinking_ref.rest_1_
  95.7 0.0 copy-start.3
  95.7 6.7 %collective-permute-done.climbing_ref.rest_0_ = bf16[128,4224]{1,0:T(8,128)(2,1)S(1)} collective-permute-done((bf16[128,4224]{1,0:T(8,128)(2,1)}, bf16[128,4224]{1,0:T(8,128)(2,1)S(1)}, u32[]{:S(2)}, u32[]{:S(2)}) %collective-permute-start) | collective-permute-done | bytes 1081376 | tf_op jit(solution)/shard_map/ppermute | solution.py:341
  102.4 0.0 copy-start
  102.4 0.0 copy-done.3
  102.4 1.0 copy-done
  103.4 2.6 %trim.4 = (bf16[128,3840]{1,0:T(8,128)(2,1)}, bf16[128,2560]{1,0:T(8,128)(2,1)}) custom-call(f32[512,512]{1,0:T(8,128)} %get-tuple-element.22.a_in.after_ref, bf16[128,4224]{1,0:T(8,128)(2,1)} %copy-done, bf16[128,2560]{1,0:T(8,128)(2,1)} %copy-done.3), custom_call_target="tpu_custom_call" | custom-call | tf_op jit(solution)/shard_map/trim/pallas_call | solution.py:331
  106.0 1.9 %collective-permute-start.3 = (bf16[128,2560]{1,0:T(8,128)(2,1)}, bf16[128,2560]{1,0:T(8,128)(2,1)S(1)}, u32[]{:S(2)}, u32[]{:S(2)}) collective-permute-start(bf16[128,2560]{1,0:T(8,128)(2,1)} %get-tuple-element.30), channel_id=1, source_target_pairs={{1,0},{2,1},{3,2},{5,4},{6,5},{7,6},{9,8},{10,9},{11,10},{13,12},{... | collective-permute-start | bytes 1966088 | tf_op jit(solution)/shard_map/ppermute | solution.py:342
  107.9 3.5 %collective-permute-start.2 = (bf16[128,3840]{1,0:T(8,128)(2,1)}, bf16[128,3840]{1,0:T(8,128)(2,1)S(1)}, u32[]{:S(2)}, u32[]{:S(2)}) collective-permute-start(bf16[128,3840]{1,0:T(8,128)(2,1)} %get-tuple-element.29), channel_id=1, source_target_pairs={{0,1},{1,2},{2,3},{4,5},{5,6},{6,7},{8,9},{9,10},{10,11},{12,13},{... | collective-permute-start | bytes 2949128 | tf_op jit(solution)/shard_map/ppermute | solution.py:341
  111.5 18.9 %factor_end.1 = (bf16[384,512]{1,0:T(8,128)(2,1)}, bf16[384,512]{1,0:T(8,128)(2,1)}) custom-call(bf16[512,512]{1,0:T(8,128)(2,1)} %all_gather.3.head_ref.after_ref, bf16[128,4608]{1,0:T(8,128)(2,1)} %get-tuple-element.21.below_ref.climbing_ref.sinking_ref, f32[512,512]{1,0:T(8,128)} %get-tuple-element.22.a_in.after_ref, f32[512,512]{1,0:T(8,128)} %get-tuple-element.23.e_in, ...), custom_call_target="tpu_custom_call" | custom-call | flops 15000000512 | bytes 4000000 | tf_op jit(solution)/shard_map/factor_end/pallas_call | solution.py:358
  130.4 0.0 collective-permute-done.3.sinking_ref.rest_3_
  130.4 0.0 copy-start.2
  130.4 0.0 collective-permute-done.2.climbing_ref.rest_2_
  130.4 0.0 copy-start.1
  130.4 0.8 copy-done.2
  131.3 0.3 copy-done.1
  131.6 2.6 %trim.5 = (bf16[128,3456]{1,0:T(8,128)(2,1)}, bf16[128,2560]{1,0:T(8,128)(2,1)}) custom-call(bf16[384,512]{1,0:T(8,128)(2,1)} %get-tuple-element.25.after_ref.high_ref, bf16[128,3840]{1,0:T(8,128)(2,1)} %copy-done.1, bf16[128,2560]{1,0:T(8,128)(2,1)} %copy-done.2), custom_call_target="tpu_custom_call" | custom-call | tf_op jit(solution)/shard_map/trim/pallas_call | solution.py:331
  134.2 2.0 %collective-permute-start.4 = (bf16[128,3456]{1,0:T(8,128)(2,1)}, bf16[128,3456]{1,0:T(8,128)(2,1)S(1)}, u32[]{:S(2)}, u32[]{:S(2)}) collective-permute-start(bf16[128,3456]{1,0:T(8,128)(2,1)} %get-tuple-element.31), channel_id=1, source_target_pairs={{0,1},{1,2},{2,3},{4,5},{5,6},{6,7},{8,9},{9,10},{10,11},{12,13},{... | collective-permute-start | bytes 2654216 | tf_op jit(solution)/shard_map/ppermute | solution.py:341
  136.1 3.4 %collective-permute-start.5 = (bf16[128,2560]{1,0:T(8,128)(2,1)}, bf16[128,2560]{1,0:T(8,128)(2,1)S(1)}, u32[]{:S(2)}, u32[]{:S(2)}) collective-permute-start(bf16[128,2560]{1,0:T(8,128)(2,1)} %get-tuple-element.32), channel_id=1, source_target_pairs={{1,0},{2,1},{3,2},{5,4},{6,5},{7,6},{9,8},{10,9},{11,10},{13,12},{... | collective-permute-start | bytes 1966088 | tf_op jit(solution)/shard_map/ppermute | solution.py:342
  139.5 7.3 %schur_near.1.rest_2_ = f32[2,384,768]{2,1,0:T(8,128)} custom-call(s32[2]{0:T(128)} %pad_add_fusion.ids_ref, bf16[384,512]{1,0:T(8,128)(2,1)} %get-tuple-element.25.after_ref.high_ref, bf16[384,512]{1,0:T(8,128)(2,1)} %get-tuple-element.26.low_ref, bf16[128,4608]{1,0:T(8,128)(2,1)} %get-tuple-element.21.below_ref.climbing_ref.sinking_ref, ...), custom_call_target="tpu_custom_call" | custom-call | flops 2000000000 | bytes 4000000 | tf_op jit(solution)/shard_map/schur_near/pallas_call | solution.py:375
  146.8 2.2 %collective-permute-done.5.rest_1_ = bf16[128,2560]{1,0:T(8,128)(2,1)S(1)} collective-permute-done((bf16[128,2560]{1,0:T(8,128)(2,1)}, bf16[128,2560]{1,0:T(8,128)(2,1)S(1)}, u32[]{:S(2)}, u32[]{:S(2)}) %collective-permute-start.5) | collective-permute-done | bytes 655392 | tf_op jit(solution)/shard_map/ppermute | solution.py:342
  149.0 0.0 copy-start.5
  149.0 3.2 %collective-permute-done.4.rest_0_ = bf16[128,3456]{1,0:T(8,128)(2,1)S(1)} collective-permute-done((bf16[128,3456]{1,0:T(8,128)(2,1)}, bf16[128,3456]{1,0:T(8,128)(2,1)S(1)}, u32[]{:S(2)}, u32[]{:S(2)}) %collective-permute-start.4) | collective-permute-done | bytes 884768 | tf_op jit(solution)/shard_map/ppermute | solution.py:341
  152.2 0.0 copy-done.5
  152.2 0.0 copy-start.4
  152.2 0.9 copy-done.4
  153.1 4.4 %schur_far.1 = (f32[384,768]{1,0:T(8,128)}, f32[384,768]{1,0:T(8,128)}) custom-call(s32[2]{0:T(128)} %pad_add_fusion.ids_ref, bf16[384,512]{1,0:T(8,128)(2,1)} %get-tuple-element.25.after_ref.high_ref, bf16[384,512]{1,0:T(8,128)(2,1)} %get-tuple-element.26.low_ref, bf16[128,4608]{1,0:T(8,128)(2,1)} %get-tuple-element.21.below_ref.climbing_ref.sinking_ref, ...), custom_call_target="tpu_custom_call" | custom-call | flops 2000000000 | bytes 4000000 | tf_op jit(solution)/shard_map/schur_far/pallas_call | solution.py:375
  157.6 6.1 %collective-permute-start.6 = (f32[384,768]{1,0:T(8,128)}, f32[384,768]{1,0:T(8,128)S(1)}, u32[]{:S(2)}, u32[]{:S(2)}) collective-permute-start(f32[384,768]{1,0:T(8,128)} %get-tuple-element.34), channel_id=1, source_target_pairs={{0,4},{4,0},{8,12},{12,8},{16,20},{20,16},{24,28},{28,24},{1,5},{5... | collective-permute-start | bytes 3538952 | tf_op jit(solution)/shard_map/ppermute | solution.py:388
  163.7 2.7 %collective-permute-done.6 = f32[384,768]{1,0:T(8,128)S(1)} collective-permute-done((f32[384,768]{1,0:T(8,128)}, f32[384,768]{1,0:T(8,128)S(1)}, u32[]{:S(2)}, u32[]{:S(2)}) %collective-permute-start.6) | collective-permute-done | bytes 1179680 | tf_op jit(solution)/shard_map/ppermute | solution.py:388
  166.4 2.4 %add_bitcast_fusion = f32[1,384,768]{2,1,0:T(8,128)} fusion(f32[384,768]{1,0:T(8,128)} %get-tuple-element.33, f32[384,768]{1,0:T(8,128)S(1)} %collective-permute-done.6), kind=kLoop, calls=%fused_computation | loop fusion | flops 294912 | bytes 3538944 | tf_op jit(solution)/shard_map/broadcast_in_dim | solution.py:389
Async XLA Ops:
  4.1 47.6 %all-to-all-start = ((bf16[8,1808,128]{2,1,0:T(8,128)(2,1)}), bf16[8,1808,128]{2,1,0:T(8,128)(2,1)}, u32[]{:S(2)}, u32[]{:S(2)}) async-start(bf16[8,1808,128]{2,1,0:T(8,128)(2,1)} %pack.1), calls=%async_computation | async-start | bytes 7405568 | tf_op jit(solution)/shard_map/all_to_all | solution.py:307
  75.0 20.7 %collective-permute-start.1 = (bf16[128,2560]{1,0:T(8,128)(2,1)}, bf16[128,2560]{1,0:T(8,128)(2,1)S(1)}, u32[]{:S(2)}, u32[]{:S(2)}) collective-permute-start(bf16[128,2560]{1,0:T(8,128)(2,1)} %get-tuple-element.28), channel_id=1, source_target_pairs={{1,0},{2,1},{3,2},{5,4},{6,5},{7,6},{9,8},{10,9},{11,10},{13,12},{... | collective-permute-start | bytes 1966088 | tf_op jit(solution)/shard_map/ppermute | solution.py:342
  78.7 23.7 %collective-permute-start = (bf16[128,4224]{1,0:T(8,128)(2,1)}, bf16[128,4224]{1,0:T(8,128)(2,1)S(1)}, u32[]{:S(2)}, u32[]{:S(2)}) collective-permute-start(bf16[128,4224]{1,0:T(8,128)(2,1)} %get-tuple-element.27), channel_id=1, source_target_pairs={{0,1},{1,2},{2,3},{4,5},{5,6},{6,7},{8,9},{9,10},{10,11},{12,13},{... | collective-permute-start | bytes 3244040 | tf_op jit(solution)/shard_map/ppermute | solution.py:341
  95.7 6.7 %copy-start.3 = (bf16[128,2560]{1,0:T(8,128)(2,1)}, bf16[128,2560]{1,0:T(8,128)(2,1)S(1)}, u32[]{:S(2)}) copy-start(bf16[128,2560]{1,0:T(8,128)(2,1)S(1)} %collective-permute-done.1.sinking_ref.rest_1_) | copy-start | bytes 1966084
  102.4 1.0 copy-start
  106.0 24.4 %collective-permute-start.3 = (bf16[128,2560]{1,0:T(8,128)(2,1)}, bf16[128,2560]{1,0:T(8,128)(2,1)S(1)}, u32[]{:S(2)}, u32[]{:S(2)}) collective-permute-start(bf16[128,2560]{1,0:T(8,128)(2,1)} %get-tuple-element.30), channel_id=1, source_target_pairs={{1,0},{2,1},{3,2},{5,4},{6,5},{7,6},{9,8},{10,9},{11,10},{13,12},{... | collective-permute-start | bytes 1966088 | tf_op jit(solution)/shard_map/ppermute | solution.py:342
  107.9 22.5 %collective-permute-start.2 = (bf16[128,3840]{1,0:T(8,128)(2,1)}, bf16[128,3840]{1,0:T(8,128)(2,1)S(1)}, u32[]{:S(2)}, u32[]{:S(2)}) collective-permute-start(bf16[128,3840]{1,0:T(8,128)(2,1)} %get-tuple-element.29), channel_id=1, source_target_pairs={{0,1},{1,2},{2,3},{4,5},{5,6},{6,7},{8,9},{9,10},{10,11},{12,13},{... | collective-permute-start | bytes 2949128 | tf_op jit(solution)/shard_map/ppermute | solution.py:341
  130.4 0.8 copy-start.2
  130.4 1.2 copy-start.1
  134.2 18.0 %collective-permute-start.4 = (bf16[128,3456]{1,0:T(8,128)(2,1)}, bf16[128,3456]{1,0:T(8,128)(2,1)S(1)}, u32[]{:S(2)}, u32[]{:S(2)}) collective-permute-start(bf16[128,3456]{1,0:T(8,128)(2,1)} %get-tuple-element.31), channel_id=1, source_target_pairs={{0,1},{1,2},{2,3},{4,5},{5,6},{6,7},{8,9},{9,10},{10,11},{12,13},{... | collective-permute-start | bytes 2654216 | tf_op jit(solution)/shard_map/ppermute | solution.py:341
  136.1 12.8 %collective-permute-start.5 = (bf16[128,2560]{1,0:T(8,128)(2,1)}, bf16[128,2560]{1,0:T(8,128)(2,1)S(1)}, u32[]{:S(2)}, u32[]{:S(2)}) collective-permute-start(bf16[128,2560]{1,0:T(8,128)(2,1)} %get-tuple-element.32), channel_id=1, source_target_pairs={{1,0},{2,1},{3,2},{5,4},{6,5},{7,6},{9,8},{10,9},{11,10},{13,12},{... | collective-permute-start | bytes 1966088 | tf_op jit(solution)/shard_map/ppermute | solution.py:342
  149.0 3.2 %copy-start.5 = (bf16[128,2560]{1,0:T(8,128)(2,1)}, bf16[128,2560]{1,0:T(8,128)(2,1)S(1)}, u32[]{:S(2)}) copy-start(bf16[128,2560]{1,0:T(8,128)(2,1)S(1)} %collective-permute-done.5.rest_1_) | copy-start | bytes 1966084
  152.2 0.9 copy-start.4
  157.6 8.8 %collective-permute-start.6 = (f32[384,768]{1,0:T(8,128)}, f32[384,768]{1,0:T(8,128)S(1)}, u32[]{:S(2)}, u32[]{:S(2)}) collective-permute-start(f32[384,768]{1,0:T(8,128)} %get-tuple-element.34), channel_id=1, source_target_pairs={{0,4},{4,0},{8,12},{12,8},{16,20},{20,16},{24,28},{28,24},{1,5},{5... | collective-permute-start | bytes 3538952 | tf_op jit(solution)/shard_map/ppermute | solution.py:388
